TPU v7x, 512 devices: a whole 4x8x8 slice. The times are simulated.
512 devices in a mesh: node: 64 (over y_lo, z, core), win: 8 (over y_hi, x).
Axes of the slice: x: 4, y: 8 (y_hi: 2, y_lo: 4; y = y_hi * 4 + y_lo), z: 8, core: 2. Of those that a mesh axis runs over, the one named last changes fastest.
Arguments:
- features: bfloat16 [32768, 8, 2, 128], P('node', 'win'), may hold values from -6 to 6
- node_vectors: float32 [32768, 128], P('node'), may hold values from -0.3 to 0.3
- projections: float32 [2, 64, 64], replicated, may hold values from -0.75 to 0.75
- mix_weight: bfloat16 [3, 128, 128], replicated, may hold values from -0.3125 to 0.3125
- region_sizes: int32 [128], replicated, may hold values from 1 to 4, 256 in all
- cotangent: bfloat16 [32768, 8, 2, 128], P('node', 'win'), may hold values from -6 to 6
Outputs:
- layer_output: bfloat16 [32768, 8, 2, 128], P('node', 'win')
- vector_grad: float32 [32768, 128], P('node')
- weight_grad: float32 [3, 128, 128], replicated
Inputs may be any that keep to these rules, and one draw needn't show every extreme that they name: `region_sizes`: each entry is a region size in units of 128 nodes; the entries sum to 256, and the largest region has 512 nodes.
All inputs are finite; a program needn't handle non-finite values.
Results may differ from a plain program's by a relative error of at most 0.015.
Values may be sent and summed in bfloat16 or wider, within the bound.
No kernel may reach another device: no remote copies, remote signals or barrier semaphores. Data moves between devices by JAX's collectives and lax.ppermute only.
A program may use at most 64 MiB of HBM per device.

v0:
```python
from functools import partial
import math

import jax
import jax.numpy as jnp
from jax import lax
from jax.sharding import PartitionSpec as P

BLOCK = 128


KEEP_INPUT = 0.05
ROWS_DIMS = (((1,), (1,)), ((), ()))
COLS_DIMS = (((0,), (0,)), ((), ()))


def padded(cells, sides, width):
    for axis, dim in sides:
        count = lax.axis_size(axis)
        ends = count - 1
        head = lax.slice_in_dim(cells, 0, width, axis=dim)
        tail = lax.slice_in_dim(cells, cells.shape[dim] - width, cells.shape[dim], axis=dim)
        cells = jnp.concatenate(
            [
                lax.ppermute(tail, axis, [(i, (i + 1) % count) for i in range(ends)]),
                cells,
                lax.ppermute(head, axis, [((i + 1) % count, i) for i in range(ends)]),
            ],
            axis=dim,
        )
    return cells


def shifted(block, axis, distance):
    devices = range(lax.axis_size(axis))
    route = [(i - distance, i) for i in devices if i - distance in devices]
    return lax.ppermute(block, axis, route)


def swapped(vectors):
    emb_half = vectors.shape[1] // 2
    return jnp.concatenate([vectors[:, emb_half:], -vectors[:, :emb_half]], axis=1)


def node_regions(region_sizes, node_index, node_total):
    region_ends = jnp.cumsum(region_sizes) * BLOCK
    region_index = jnp.sum((region_ends[None, :] <= node_index[:, None]).astype(jnp.int32), axis=1)
    in_range = (node_index >= 0) & (node_index < node_total)
    return jnp.where(in_range, region_index, -1)


def node_rim(values):
    return padded(values, (("node", 0),), values.shape[0])


def node_pass(values, offset_by):
    return shifted(values.astype(jnp.bfloat16), "node", offset_by).astype(values.dtype)


def spread_back(parts, node_count):
    lower = parts[:node_count]
    middle = parts[node_count : 2 * node_count]
    upper = parts[2 * node_count :]
    return middle + node_pass(lower, -1) + node_pass(upper, 1)


def dense_product(adj_rounded, wide_rows):
    return jnp.dot(adj_rounded, wide_rows, preferred_element_type=jnp.float32)


def body(features, node_vectors, projections, mix_weight, region_sizes, cotangent):
    node_count = features.shape[0]
    windows_dev = features.shape[1]
    steps_dev = features.shape[2]
    channels = features.shape[3]
    row_width = windows_dev * steps_dev * channels
    emb_half = node_vectors.shape[1] // 2
    node_total = node_count * lax.axis_size("node")
    first_node = lax.axis_index("node") * node_count
    own_index = first_node + jnp.arange(node_count, dtype=jnp.int32)
    wide_index = first_node - node_count + jnp.arange(3 * node_count, dtype=jnp.int32)
    own_region = node_regions(region_sizes, own_index, node_total)
    wide_region = node_regions(region_sizes, wide_index, node_total)
    highest = lax.Precision.HIGHEST
    source_m = jnp.tanh(
        3.0
        * jnp.dot(
            node_vectors[:, :emb_half],
            projections[0],
            precision=highest,
            preferred_element_type=jnp.float32,
        )
    )
    target_m = jnp.tanh(
        3.0
        * jnp.dot(
            node_vectors[:, emb_half:],
            projections[1],
            precision=highest,
            preferred_element_type=jnp.float32,
        )
    )
    learned = jnp.concatenate([source_m, target_m], axis=1).astype(jnp.bfloat16)
    inputs = features.reshape(node_count, row_width)
    rim_block = node_rim(jnp.concatenate([inputs, learned], axis=1))
    wide_inputs = rim_block[:, :row_width]
    wide_learned = rim_block[:, row_width:]
    scores = lax.dot_general(
        learned, swapped(wide_learned), ROWS_DIMS, preferred_element_type=jnp.float32
    )
    same_region = (own_region[:, None] == wide_region[None, :]) & (wide_region[None, :] >= 0)
    squashed = jnp.tanh(3.0 * scores)
    positive = jnp.maximum(squashed, 0.0)
    adjacency = jnp.where(same_region, positive * positive, 0.0)
    degree = 1.0 + jnp.sum(adjacency, axis=1)
    identity = (own_index[:, None] == wide_index[None, :]).astype(jnp.float32)
    adj_rounded = (adjacency + identity).astype(jnp.bfloat16)
    propagate = partial(dense_product, adj_rounded)
    inputs_f = inputs.astype(jnp.float32)
    prop_one = propagate(wide_inputs) / degree[:, None]
    hop_one = (KEEP_INPUT * inputs_f + (1.0 - KEEP_INPUT) * prop_one).astype(jnp.bfloat16)
    wide_one = node_rim(hop_one)
    prop_two = propagate(wide_one) / degree[:, None]
    hop_two = (KEEP_INPUT * inputs_f + (1.0 - KEEP_INPUT) * prop_two).astype(jnp.bfloat16)
    row_count = node_count * windows_dev * steps_dev
    hop_list = (inputs, hop_one, hop_two)
    mixed = jnp.zeros((row_count, channels), jnp.float32)
    for hop_order in range(3):
        mixed = mixed + jnp.dot(
            hop_list[hop_order].reshape(row_count, channels),
            mix_weight[hop_order],
            preferred_element_type=jnp.float32,
        )
    layer_output = mixed.astype(jnp.bfloat16).reshape(features.shape)
    upstream = cotangent.reshape(row_count, channels)
    norm_scale = 1.0 / math.sqrt(row_count * lax.axis_size("node") * lax.axis_size("win"))
    partial_mix = (
        jnp.stack(
            [
                lax.dot_general(
                    layer_rows.reshape(row_count, channels),
                    upstream,
                    COLS_DIMS,
                    preferred_element_type=jnp.float32,
                )
                for layer_rows in hop_list
            ]
        )
        * norm_scale
    )
    weight_grad = lax.psum(partial_mix, ("node", "win"))
    back_two = lax.dot_general(
        upstream, mix_weight[2], ROWS_DIMS, preferred_element_type=jnp.float32
    ).reshape(node_count, row_width)
    grad_two = ((1.0 - KEEP_INPUT) * back_two / degree[:, None]).astype(jnp.bfloat16)
    partials = lax.dot_general(adj_rounded, grad_two, COLS_DIMS, preferred_element_type=jnp.float32)
    carried = spread_back(partials, node_count)
    back_one = (
        lax.dot_general(
            upstream, mix_weight[1], ROWS_DIMS, preferred_element_type=jnp.float32
        ).reshape(node_count, row_width)
        + carried
    )
    grad_one = ((1.0 - KEEP_INPUT) * back_one / degree[:, None]).astype(jnp.bfloat16)
    pair_inner = lax.dot_general(
        jnp.concatenate([grad_one, grad_two], axis=1),
        jnp.concatenate([wide_inputs, wide_one], axis=1),
        ROWS_DIMS,
        preferred_element_type=jnp.float32,
    )
    offset = jnp.sum(grad_one.astype(jnp.float32) * prop_one, axis=1) + jnp.sum(
        grad_two.astype(jnp.float32) * prop_two, axis=1
    )
    score_grad = jnp.where(
        same_region,
        6.0 * (pair_inner - offset[:, None]) * positive * (1.0 - squashed * squashed),
        0.0,
    ).astype(jnp.bfloat16)
    row_part = jnp.dot(score_grad, swapped(wide_learned), preferred_element_type=jnp.float32)
    column_part = -lax.dot_general(
        score_grad, swapped(learned), COLS_DIMS, preferred_element_type=jnp.float32
    )
    grad_m = row_part + spread_back(column_part, node_count)
    source_grad = jnp.dot(
        3.0 * (1.0 - source_m * source_m) * grad_m[:, :emb_half],
        projections[0].T,
        precision=highest,
        preferred_element_type=jnp.float32,
    )
    target_grad = jnp.dot(
        3.0 * (1.0 - target_m * target_m) * grad_m[:, emb_half:],
        projections[1].T,
        precision=highest,
        preferred_element_type=jnp.float32,
    )
    vector_grad = lax.psum(
        jnp.concatenate([source_grad, target_grad], axis=1).astype(jnp.bfloat16), "win"
    ).astype(jnp.float32)
    return (layer_output, vector_grad, weight_grad)


def solution(mesh):
    placed = (
        P("node", "win", None, None),
        P("node", None),
        P(),
        P(),
        P(),
        P("node", "win", None, None),
    )
    return jax.shard_map(
        body,
        mesh=mesh,
        in_specs=placed,
        out_specs=(P("node", "win", None, None), P("node", None), P()),
        check_vma=False,
    )
```

profile of v0, /device:TPU:1, one launch (start us, length us, event | category | flops | bytes accessed | tf_op | source)
XLA Modules:
  0.0 480.1 jit_solution(4617464330748801811)
XLA Ops:
  7.2 2.1 fusion.88
  9.4 2.1 fusion.83
  11.6 1.0 copy.51
  12.8 8.8 %collective-permute-start.1 = (bf16[512,384]{1,0:T(8,128)(2,1)S(1)}, bf16[512,384]{1,0:T(8,128)(2,1)S(1)}, u32[]{:S(2)}, u32[]{:S(2)}) collective-permute-start(bf16[512,384]{1,0:T(8,128)(2,1)S(1)} %pad_maximum_fusion.1), channel_id=1, source_target_pairs={{8,0},{16,8},{24,16},{32,24},{40,32},{48,40},{56,48},{64,56},{72,6... | collective-permute-start | bytes 1179656 | tf_op jit(solution)/shard_map/ppermute | solution.py:27
  21.6 1.9 collective-permute-start
  25.7 2.5 collective-permute-done
  28.6 3.3 fusion.6
  32.0 1.5 add_convert_fusion.2
  33.5 1.9 collective-permute-start.3
  35.4 4.4 collective-permute-start.2
  40.2 1.0 fusion.62
  41.2 1.0 collective-permute-done.3
  42.3 1.2 collective-permute-done.2
  43.4 3.5 multiply_reduce_fusion
  48.4 1.9 collective-permute-start.4
  50.3 4.4 collective-permute-start.5
  56.6 1.1 reshape.106
  57.7 2.2 convolution_add_fusion.1
  59.9 1.6 multiply_reduce_fusion.1
  61.6 2.9 fusion.5
  64.6 1.3 fusion.90
  66.6 2.0 collective-permute-start.6
  68.6 3.6 collective-permute-start.7
  73.3 1.2 collective-permute-done.7
  75.2 2.0 fusion.31
  77.2 1.1 convolution_convert_fusion
  78.2 1.0 convolution_convert_fusion.1
  81.1 1.7 fusion.14
  82.7 113.3 %all-reduce.3.cloned.1.call-done = bf16[512,128]{0,1:T(8,128)(2,1)} async-done(((bf16[512,128]{0,1:T(8,128)(2,1)}), bf16[512,128]{0,1:T(8,128)(2,1)}) %all-reduce.3.cloned.1.call-update) | async-done | bytes 131088 | tf_op jit(solution)/shard_map/psum | solution.py:196
  196.0 1.7 copy.38
  197.8 273.9 %all-reduce.5.cloned.1.call-done = f32[3,128,128]{2,1,0:T(8,128)} async-done(((f32[3,128,128]{2,1,0:T(8,128)}), f32[3,128,128]{2,1,0:T(8,128)}) %all-reduce.5.cloned.1.call-update) | async-done | bytes 196624 | tf_op jit(solution)/shard_map/psum | solution.py:151
  471.7 1.6 copy.54
  (95 shorter events, 10.7 us)
Async XLA Ops:
  7.2 17.5 %copy-start = (bf16[512,1,2,128]{3,2,1,0:T(2,128)(2,1)S(1)}, bf16[512,1,2,128]{3,2,1,0:T(2,128)(2,1)}, u32[]{:S(2)}) copy-start(bf16[512,1,2,128]{3,2,1,0:T(2,128)(2,1)} %param.11) | copy-start | bytes 786436
  7.2 16.4 %copy-start.26 = (s32[128]{0:T(128)S(1)}, s32[128]{0:T(128)}, u32[]{:S(2)}) copy-start(s32[128]{0:T(128)} %param.10) | copy-start | bytes 1540
  7.2 188.9 %all-reduce.3.cloned.1.call-start = ((), (), s32[]{:S(2)}) async-start(), calls=%async_computation | async-start | bytes 262144 | tf_op jit(solution)/shard_map/psum | solution.py:196
  9.4 19.2 %copy-start.10 = (bf16[512,64]{0,1:T(8,128)(2,1)}, bf16[512,64]{0,1:T(8,128)(2,1)S(1)}, u32[]{:S(2)}) copy-start(bf16[512,64]{0,1:T(8,128)(2,1)S(1)} %get-tuple-element.29) | copy-start | bytes 196612
  12.8 12.9 %collective-permute-start.1 = (bf16[512,384]{1,0:T(8,128)(2,1)S(1)}, bf16[512,384]{1,0:T(8,128)(2,1)S(1)}, u32[]{:S(2)}, u32[]{:S(2)}) collective-permute-start(bf16[512,384]{1,0:T(8,128)(2,1)S(1)} %pad_maximum_fusion.1), channel_id=1, source_target_pairs={{8,0},{16,8},{24,16},{32,24},{40,32},{48,40},{56,48},{64,56},{72,6... | collective-permute-start | bytes 1179656 | tf_op jit(solution)/shard_map/ppermute | solution.py:27
  21.6 6.6 %collective-permute-start = (bf16[512,384]{1,0:T(8,128)(2,1)S(1)}, bf16[512,384]{1,0:T(8,128)(2,1)S(1)}, u32[]{:S(2)}, u32[]{:S(2)}) collective-permute-start(bf16[512,384]{1,0:T(8,128)(2,1)S(1)} %pad_maximum_fusion.1), channel_id=1, source_target_pairs={{0,8},{8,16},{16,24},{24,32},{32,40},{40,48},{48,56},{56,64},{64,7... | collective-permute-start | bytes 1179656 | tf_op jit(solution)/shard_map/ppermute | solution.py:25
  24.7 3.9 copy-start.24
  28.4 28.2 %copy-start.1 = (bf16[1536,384]{1,0:T(8,128)(2,1)}, bf16[1536,384]{1,0:T(8,128)(2,1)S(1)}, u32[]{:S(2)}) copy-start(bf16[1536,384]{1,0:T(8,128)(2,1)S(1)} %pad_maximum_fusion) | copy-start | bytes 3538948
  28.6 3.4 copy-start.3
  28.6 3.4 copy-start.5
  32.0 7.8 %copy-start.14 = (bf16[3,128,128]{2,1,0:T(8,128)(2,1)S(1)}, bf16[3,128,128]{2,1,0:T(8,128)(2,1)}, u32[]{:S(2)}) copy-start(bf16[3,128,128]{2,1,0:T(8,128)(2,1)} %param.9) | copy-start | bytes 294916
  33.5 8.7 %collective-permute-start.3 = (bf16[512,256]{1,0:T(8,128)(2,1)}, bf16[512,256]{1,0:T(8,128)(2,1)}, u32[]{:S(2)}, u32[]{:S(2)}) collective-permute-start(bf16[512,256]{1,0:T(8,128)(2,1)} %get-tuple-element.33), channel_id=1, source_target_pairs={{8,0},{16,8},{24,16},{32,24},{40,32},{48,40},{56,48},{64,56},{72,6... | collective-permute-start | bytes 786440 | tf_op jit(solution)/shard_map/ppermute | solution.py:27
  35.4 8.0 %collective-permute-start.2 = (bf16[512,256]{1,0:T(8,128)(2,1)}, bf16[512,256]{1,0:T(8,128)(2,1)}, u32[]{:S(2)}, u32[]{:S(2)}) collective-permute-start(bf16[512,256]{1,0:T(8,128)(2,1)} %get-tuple-element.33), channel_id=1, source_target_pairs={{0,8},{8,16},{16,24},{24,32},{32,40},{40,48},{48,56},{56,64},{64,7... | collective-permute-start | bytes 786440 | tf_op jit(solution)/shard_map/ppermute | solution.py:25
  41.2 5.7 %copy-start.7 = (bf16[512,1536]{1,0:T(8,128)(2,1)S(1)}, bf16[512,1536]{1,0:T(8,128)(2,1)}, u32[]{:S(2)}) copy-start(bf16[512,1536]{1,0:T(8,128)(2,1)} %copy-done.6) | copy-start | bytes 4718596
  46.9 7.8 %copy-start.9 = (bf16[512,1,2,128]{3,2,1,0:T(2,128)(2,1)S(1)}, bf16[512,1,2,128]{3,2,1,0:T(2,128)(2,1)}, u32[]{:S(2)}) copy-start(bf16[512,1,2,128]{3,2,1,0:T(2,128)(2,1)} %param.6) | copy-start | bytes 786436
  48.4 11.6 %collective-permute-start.4 = (bf16[512,256]{1,0:T(8,128)(2,1)}, bf16[512,256]{1,0:T(8,128)(2,1)}, u32[]{:S(2)}, u32[]{:S(2)}) collective-permute-start(bf16[512,256]{1,0:T(8,128)(2,1)} %get-tuple-element.24), channel_id=1, source_target_pairs={{8,0},{16,8},{24,16},{32,24},{40,32},{48,40},{56,48},{64,56},{72,6... | collective-permute-start | bytes 786440 | tf_op jit(solution)/shard_map/ppermute | solution.py:37
  50.3 9.6 %collective-permute-start.5 = (bf16[512,256]{1,0:T(8,128)(2,1)}, bf16[512,256]{1,0:T(8,128)(2,1)}, u32[]{:S(2)}, u32[]{:S(2)}) collective-permute-start(bf16[512,256]{1,0:T(8,128)(2,1)} %get-tuple-element.25), channel_id=1, source_target_pairs={{0,8},{8,16},{16,24},{24,32},{32,40},{40,48},{48,56},{56,64},{64,7... | collective-permute-start | bytes 786440 | tf_op jit(solution)/shard_map/ppermute | solution.py:37
  56.5 5.0 %copy-start.23 = (f32[512]{0:T(512)S(1)}, f32[512]{0:T(512)}, u32[]{:S(2)}) copy-start(f32[512]{0:T(512)} %get-tuple-element.14) | copy-start | bytes 6148
  56.5 5.0 %slice-start = ((bf16[1536,384]{1,0:T(8,128)(2,1)}), bf16[1536,256]{1,0:T(8,128)(2,1)S(1)}, s32[]{:S(2)}) async-start(bf16[1536,384]{1,0:T(8,128)(2,1)} %copy-done.1), calls=%async_computation.2 | async-start | bytes 1572864 | tf_op jit(solution)/shard_map/slice | solution.py:106
  56.5 5.0 %copy-start.16 = (bf16[512,256]{1,0:T(8,128)(2,1)S(1)}, bf16[512,256]{1,0:T(8,128)(2,1)}, u32[]{:S(2)}) copy-start(bf16[512,256]{1,0:T(8,128)(2,1)} %copy-done.15) | copy-start | bytes 786436
  57.7 3.9 copy-start.25
  57.7 3.9 copy-start.27
  64.5 8.6 %copy-start.18 = (bf16[512,256]{1,0:T(8,128)(2,1)S(1)}, bf16[512,256]{1,0:T(8,128)(2,1)}, u32[]{:S(2)}) copy-start(bf16[512,256]{1,0:T(8,128)(2,1)} %get-tuple-element.26) | copy-start | bytes 786436
  64.5 10.6 %copy-start.4 = (bf16[1536,64]{1,0:T(8,128)(2,1)S(1)}, bf16[1536,64]{1,0:T(8,128)(2,1)}, u32[]{:S(2)}) copy-start(bf16[1536,64]{1,0:T(8,128)(2,1)} %copy-done.3) | copy-start | bytes 589828
  65.8 11.3 %copy-start.13 = (f32[512,64]{0,1:T(8,128)S(1)}, f32[512,64]{0,1:T(8,128)}, u32[]{:S(2)}) copy-start(f32[512,64]{0,1:T(8,128)} %get-tuple-element.30) | copy-start | bytes 393220
  66.6 11.7 %copy-start.12 = (f32[512,64]{0,1:T(8,128)S(1)}, f32[512,64]{0,1:T(8,128)}, u32[]{:S(2)}) copy-start(f32[512,64]{0,1:T(8,128)} %get-tuple-element.31) | copy-start | bytes 393220
  66.6 6.7 %collective-permute-start.6 = (bf16[512,128]{0,1:T(8,128)(2,1)}, bf16[512,128]{0,1:T(8,128)(2,1)S(1)}, u32[]{:S(2)}, u32[]{:S(2)}) collective-permute-start(bf16[512,128]{0,1:T(8,128)(2,1)} %get-tuple-element.27), channel_id=1, source_target_pairs={{8,0},{16,8},{24,16},{32,24},{40,32},{48,40},{56,48},{64,56},{72,6... | collective-permute-start | bytes 393224 | tf_op jit(solution)/shard_map/ppermute | solution.py:37
  68.6 5.9 %collective-permute-start.7 = (bf16[512,128]{0,1:T(8,128)(2,1)}, bf16[512,128]{0,1:T(8,128)(2,1)S(1)}, u32[]{:S(2)}, u32[]{:S(2)}) collective-permute-start(bf16[512,128]{0,1:T(8,128)(2,1)} %get-tuple-element.28), channel_id=1, source_target_pairs={{0,8},{8,16},{16,24},{24,32},{32,40},{40,48},{48,56},{56,64},{64,7... | collective-permute-start | bytes 393224 | tf_op jit(solution)/shard_map/ppermute | solution.py:37
  75.2 5.1 %copy-start.19 = (f32[1,128,128]{2,1,0:T(8,128)S(1)}, f32[1,128,128]{2,1,0:T(8,128)}, u32[]{:S(2)}) copy-start(f32[1,128,128]{2,1,0:T(8,128)} %convolution_bitcast_fusion.1) | copy-start | bytes 196612
  75.2 5.2 %copy-start.22 = (f32[1,128,128]{2,1,0:T(8,128)S(1)}, f32[1,128,128]{2,1,0:T(8,128)}, u32[]{:S(2)}) copy-start(f32[1,128,128]{2,1,0:T(8,128)} %convolution_bitcast_fusion.2) | copy-start | bytes 196612
  75.2 5.9 %copy-start.2 = (f32[1024,128]{1,0:T(8,128)S(1)}, f32[1024,128]{1,0:T(8,128)}, u32[]{:S(2)}) copy-start(f32[1024,128]{1,0:T(8,128)} %convolution_add_fusion.1) | copy-start | bytes 1572868
  80.0 391.7 %all-reduce.5.cloned.1.call-start = ((), (), s32[]{:S(2)}) async-start(), calls=%async_computation.1 | async-start | bytes 393216 | tf_op jit(solution)/shard_map/psum | solution.py:151
  (7 other events, 14.2 us)
Sparse Core Ops, SparseCore 0:
  80.1 115.9 all-reduce.2
  201.6 270.0 all-reduce.4
where the time goes:
time: 481 us; the launch traced here: 480 us
  waiting for transfers between devices  393 us (82%)
  matrix products  29.5 us (6%)
  starting transfers between devices  29 us (6%)
  between operations  14.6 us (3%)
  local copies, waits for them, and re-layouts  9.33 us (2%)
    psum x1, waiting for transfers between devices, body(): weight_grad = lax.psum(partial_mix, ('node', 'win'))  274 us
    psum x1, waiting for transfers between devices, body(): lax.psum(jnp.concatenate([source_grad, target_grad], axis=1).astype(jnp.b...  113 us
    ppermute x4, starting transfers between devices, shifted(): return lax.ppermute(block, axis, route)  12 us
    ppermute x2, starting transfers between devices, padded(): lax.ppermute(head, axis, [((i + 1) % count, i) for i in range(ends)])  10.7 us
  transfers between devices with their start and end apart: 10, of which 6 were waited for; matrix products, arithmetic and copies ran while one was open for 3% of the time, Pallas kernels for 0%

commit v1 on v0

v1 whole, which is shorter than its diff:
```python
from functools import partial
import math

import jax
import jax.numpy as jnp
from jax import lax
from jax.experimental import pallas as pl
from jax.experimental.pallas import tpu as pltpu
from jax.sharding import PartitionSpec as P

BLOCK = 128
HALO = 3
KEEP_INPUT = 0.05
F32 = jnp.float32
BF16 = jnp.bfloat16
NT = (((1,), (1,)), ((), ()))
TN = (((0,), (0,)), ((), ()))
HIGHEST = lax.Precision.HIGHEST


def block_diagonal(projections):
    zero = jnp.zeros_like(projections[0])
    return jnp.concatenate(
        [
            jnp.concatenate([projections[0], zero], axis=1),
            jnp.concatenate([zero, projections[1]], axis=1),
        ],
        axis=0,
    )


def pack_kernel(x_ref, g_ref, nv_ref, proj_ref, head_ref, tail_ref, m_ref, flat_ref):
    nodes, width = nv_ref.shape
    rim = head_ref.shape[0]
    learned = jnp.tanh(
        3.0
        * jnp.dot(
            nv_ref[...],
            block_diagonal(proj_ref[...]),
            precision=HIGHEST,
            preferred_element_type=F32,
        )
    )
    m_ref[...] = learned
    rounded = learned.astype(BF16)
    head_ref[:, 4 * width :] = rounded[:rim]
    tail_ref[:, 4 * width :] = rounded[nodes - rim :]
    for part, source in enumerate((x_ref, g_ref)):
        flat_ref[...] = source[...].astype(F32)
        for step in range(2):
            rows = flat_ref[pl.ds(step, nodes, stride=2), :].astype(BF16)
            columns = pl.ds((2 * part + step) * width, width)
            head_ref[:, columns] = rows[:rim]
            tail_ref[:, columns] = rows[nodes - rim :]


def layer_kernel(
    norm_scale,
    region_ref,
    low_ref,
    high_ref,
    head_ref,
    tail_ref,
    m_ref,
    proj_ref,
    mix_ref,
    out_ref,
    sums_ref,
    x_ref,
    g_ref,
    learned_ref,
    swapped_ref,
    adj_ref,
    adjt_ref,
    score_ref,
    rdeg_ref,
    one_ref,
    q_one_ref,
    q_two_ref,
    off_ref,
    offrow_ref,
    flat_ref,
):
    b = BLOCK
    nodes, width = m_ref.shape
    rim = head_ref.shape[0]
    own_units = nodes // b
    units = own_units + 2 * HALO
    row = 2 * width
    pieces = (
        (0, low_ref, 0, rim),
        (rim, head_ref, 0, rim),
        (2 * rim, tail_ref, 2 * rim - nodes, nodes - rim),
        (rim + nodes, high_ref, 0, rim),
    )
    for start, source, first, count in pieces:
        x_ref[start : start + count, :] = source[first : first + count, :row]
        g_ref[start : start + count, :] = source[first : first + count, row : 2 * row]
        learned_ref[start : start + count, :] = source[first : first + count, 2 * row :]
    learned = learned_ref[...]
    half = width // 2
    swapped_ref[...] = jnp.concatenate([learned[:, half:], -learned[:, :half]], axis=1)

    chunks = []
    for k in range(units // 2):
        first = max(0, 2 * k - HALO)
        last = min(units - 1, 2 * k + 1 + HALO)
        chunks.append((2 * k, first, last - first + 1))

    def lanes(unit_first, unit_count):
        return slice(unit_first * b, (unit_first + unit_count) * b)

    regions = [region_ref[u] for u in range(units)]
    eye = (
        lax.broadcasted_iota(jnp.int32, (b, b), 0) == lax.broadcasted_iota(jnp.int32, (b, b), 1)
    ).astype(F32)
    own_first = HALO
    for u in range(own_units):
        for v in range(units):
            lo, hi = 0, 0
            for r, c, w in chunks:
                if r <= u + own_first < r + 2:
                    lo, hi = c, c + w
            if not lo <= v < hi:
                score_ref[lanes(u, 1), lanes(v, 1)] = jnp.zeros((b, b), F32)
    for r, c, w in chunks:
        scores = lax.dot_general(
            learned_ref[lanes(r, 2), :],
            swapped_ref[lanes(c, w), :],
            NT,
            preferred_element_type=F32,
        )
        for i in range(2):
            u = r + i
            mask = jnp.concatenate(
                [
                    jnp.full(
                        (1, b),
                        jnp.where((regions[u] == regions[v]) & (regions[u] >= 0), 1.0, 0.0),
                        F32,
                    )
                    for v in range(c, c + w)
                ],
                axis=1,
            )
            squashed = jnp.tanh(3.0 * scores[i * b : (i + 1) * b]) * mask
            if own_first <= u < own_first + own_units:
                score_ref[lanes(u - own_first, 1), lanes(c, w)] = squashed
            positive = jnp.maximum(squashed, 0.0)
            negative = jnp.minimum(squashed, 0.0)
            forward = positive * positive
            backward = negative * negative
            adj_ref[lanes(u, 1), : w * b] = forward.astype(BF16)
            adjt_ref[lanes(u, 1), : w * b] = backward.astype(BF16)
            own = lanes(u - c, 1)
            adj_ref[lanes(u, 1), own] = (forward[:, own] + eye).astype(BF16)
            adjt_ref[lanes(u, 1), own] = (backward[:, own] + eye).astype(BF16)
            degree = 1.0 + jnp.sum(forward, axis=1, keepdims=True)
            rdeg_ref[lanes(u, 1), :] = jnp.broadcast_to(1.0 / degree, (b, width))

    def twice(values):
        return jnp.concatenate([values, values], axis=1)

    def per_step(rows, weight, dims):
        return jnp.concatenate(
            [
                lax.dot_general(
                    rows[:, s * width : (s + 1) * width], weight, dims, preferred_element_type=F32
                )
                for s in range(2)
            ],
            axis=1,
        )

    keep = 1.0 - KEEP_INPUT
    for r, _, _ in chunks:
        rows = lanes(r, 2)
        back_two = per_step(g_ref[rows, :], mix_ref[2], NT)
        q_two_ref[rows, :] = (keep * back_two * twice(rdeg_ref[rows, :])).astype(BF16)
    for r, c, w in chunks:
        rows = lanes(r, 2)
        carried = jnp.dot(
            adjt_ref[rows, : w * b], q_two_ref[lanes(c, w), :], preferred_element_type=F32
        )
        back_one = per_step(g_ref[rows, :], mix_ref[1], NT) + carried
        grad_one = (keep * back_one * twice(rdeg_ref[rows, :])).astype(BF16)
        q_one_ref[rows, :] = grad_one
        prop = jnp.dot(
            adj_ref[rows, : w * b], x_ref[lanes(c, w), :], preferred_element_type=F32
        ) * twice(rdeg_ref[rows, :])
        one_ref[rows, :] = (KEEP_INPUT * x_ref[rows, :].astype(F32) + keep * prop).astype(BF16)
        off_ref[rows, :] = jnp.broadcast_to(
            jnp.sum(grad_one.astype(F32) * prop, axis=1, keepdims=True), (2 * b, width)
        )
    own_start = own_first * b
    for r, c, w in chunks:
        rows = lanes(r, 2)
        prop = jnp.dot(
            adj_ref[rows, : w * b], one_ref[lanes(c, w), :], preferred_element_type=F32
        ) * twice(rdeg_ref[rows, :])
        hop_two = (KEEP_INPUT * x_ref[rows, :].astype(F32) + keep * prop).astype(BF16)
        offset = off_ref[rows, :] + jnp.broadcast_to(
            jnp.sum(q_two_ref[rows, :].astype(F32) * prop, axis=1, keepdims=True), (2 * b, width)
        )
        off_ref[rows, :] = offset
        for i in range(2):
            u = r + i
            offrow_ref[:, lanes(u, 1)] = jnp.transpose(offset[i * b : (i + 1) * b])[:8]
            if own_first <= u < own_first + own_units:
                own = lanes(u, 1)
                hops = (x_ref[own, :], one_ref[own, :], hop_two[i * b : (i + 1) * b])
                mixed = per_step(hops[0], mix_ref[0], (((1,), (0,)), ((), ())))
                for k in (1, 2):
                    mixed = mixed + per_step(hops[k], mix_ref[k], (((1,), (0,)), ((), ())))
                for s in range(2):
                    flat_ref[pl.ds(2 * (u - own_first) * b + s, b, stride=2), :] = mixed[
                        :, s * width : (s + 1) * width
                    ]
                x_two = hops[2]
                adjt_ref[own, adjt_ref.shape[1] - row :] = x_two
    out_ref[...] = flat_ref[...].astype(BF16)

    own = slice(own_start, own_start + nodes)
    groups = sums_ref.shape[0]
    rows_v = nodes // groups
    weight_rows = []
    for hop in (
        x_ref[own, :],
        one_ref[own, :],
        adjt_ref[own, adjt_ref.shape[1] - row :],
    ):
        total = jnp.zeros((width, width), F32)
        for s in range(2):
            cut = slice(s * width, (s + 1) * width)
            total = total + lax.dot_general(
                hop[:, cut], g_ref[own, cut], TN, preferred_element_type=F32
            )
        weight_rows.append((total * norm_scale).astype(BF16))
    weight_rows.append(jnp.zeros((groups * rows_v - 3 * width, width), BF16))
    weights = jnp.concatenate(weight_rows, axis=0)
    for k in range(groups):
        sums_ref[k, rows_v:, :] = weights[k * rows_v : (k + 1) * rows_v]

    diagonal = block_diagonal(proj_ref[...])
    for k in range(own_units // 2):
        c, w = 2 * k, 2 * HALO + 2
        rows = lanes(own_first + 2 * k, 2)
        columns = lanes(c, w)
        inner = lax.dot_general(
            q_one_ref[rows, :], x_ref[columns, :], NT, preferred_element_type=F32
        ) + lax.dot_general(
            q_two_ref[rows, :], one_ref[columns, :], NT, preferred_element_type=F32
        )
        inner_t = lax.dot_general(
            x_ref[rows, :], q_one_ref[columns, :], NT, preferred_element_type=F32
        ) + lax.dot_general(
            one_ref[rows, :], q_two_ref[columns, :], NT, preferred_element_type=F32
        )
        local = slice(2 * k * b, (2 * k + 2) * b)
        squashed = score_ref[local, columns]
        offset = jnp.concatenate([off_ref[rows, :]] * w, axis=1)
        chosen = jnp.where(
            squashed > 0.0, inner - offset, inner_t - offrow_ref[0:1, columns]
        )
        pair = (6.0 * squashed * (1.0 - squashed * squashed) * chosen).astype(BF16)
        grad_m = jnp.dot(pair, swapped_ref[columns, :], preferred_element_type=F32)
        mine = m_ref[local, :]
        grad = lax.dot_general(
            3.0 * (1.0 - mine * mine) * grad_m,
            diagonal,
            NT,
            precision=HIGHEST,
            preferred_element_type=F32,
        ).astype(BF16)
        per = 2 * b // rows_v
        for j in range(per):
            sums_ref[k * per + j, :rows_v, :] = grad[j * rows_v : (j + 1) * rows_v]


def device_groups(counts, kept):
    strides = [math.prod(counts[i + 1 :]) for i in range(len(counts))]

    def spread(axes):
        numbers = [0]
        for i in axes:
            numbers = [n + k * strides[i] for n in numbers for k in range(counts[i])]
        return numbers

    others = [i for i in range(len(counts)) if i not in kept]
    return [[base + k for k in spread(kept)] for base in spread(others)]


def body(features, node_vectors, projections, mix_weight, region_sizes, cotangent):
    nodes, _, steps, width = features.shape
    axes = ("node", "win")
    node_count, win_count = lax.axis_size("node"), lax.axis_size("win")
    own_units = nodes // BLOCK
    units = own_units + 2 * HALO
    rim = HALO * BLOCK
    flat = nodes * steps
    head, tail, learned = pl.pallas_call(
        pack_kernel,
        name="pack",
        out_shape=(
            jax.ShapeDtypeStruct((rim, 5 * width), BF16),
            jax.ShapeDtypeStruct((rim, 5 * width), BF16),
            jax.ShapeDtypeStruct((nodes, width), F32),
        ),
        scratch_shapes=[pltpu.VMEM((flat, width), F32)],
        compiler_params=pltpu.CompilerParams(vmem_limit_bytes=16 << 20),
    )(
        features.reshape(flat, width),
        cotangent.reshape(flat, width),
        node_vectors,
        projections,
    )
    low = lax.ppermute(tail, "node", [(i, i + 1) for i in range(node_count - 1)])
    high = lax.ppermute(head, "node", [(i + 1, i) for i in range(node_count - 1)])
    unit = lax.axis_index("node") * own_units - HALO + jnp.arange(units, dtype=jnp.int32)
    ends = jnp.cumsum(region_sizes)
    region = jnp.sum((ends[None, :] <= unit[:, None]).astype(jnp.int32), axis=1)
    in_range = (unit >= 0) & (unit < node_count * own_units)
    region = jnp.where(in_range, region, -1)

    span = units * BLOCK
    y_count, x_count = 4, win_count
    inner_count = node_count // y_count
    groups = y_count * x_count
    rows_v = nodes // groups
    band = (2 * HALO + 2) * BLOCK
    row = steps * width
    out, sums = pl.pallas_call(
        partial(layer_kernel, 1.0 / math.sqrt(flat * node_count * win_count)),
        name="layer",
        in_specs=[pl.BlockSpec(memory_space=pltpu.SMEM)]
        + [pl.BlockSpec(memory_space=pltpu.VMEM)] * 7,
        out_shape=(
            jax.ShapeDtypeStruct((flat, width), BF16),
            jax.ShapeDtypeStruct((groups, 2 * rows_v, width), BF16),
        ),
        scratch_shapes=[
            pltpu.VMEM((span, row), BF16),
            pltpu.VMEM((span, row), BF16),
            pltpu.VMEM((span, width), BF16),
            pltpu.VMEM((span, width), BF16),
            pltpu.VMEM((span, band), BF16),
            pltpu.VMEM((span, band + row), BF16),
            pltpu.VMEM((nodes, span), F32),
            pltpu.VMEM((span, width), F32),
            pltpu.VMEM((span, row), BF16),
            pltpu.VMEM((span, row), BF16),
            pltpu.VMEM((span, row), BF16),
            pltpu.VMEM((span, width), F32),
            pltpu.VMEM((8, span), F32),
            pltpu.VMEM((flat, width), F32),
        ],
        compiler_params=pltpu.CompilerParams(vmem_limit_bytes=40 << 20),
    )(region, low, high, head, tail, learned, projections, mix_weight)

    counts = (y_count, inner_count, win_count)
    outer_groups = device_groups(counts, (0, 2))
    inner_groups = device_groups(counts, (1,))
    exchange = partial(
        lax.all_to_all, axis_name=axes, split_axis=0, concat_axis=0, tiled=True
    )
    got = exchange(sums, axis_index_groups=outer_groups).astype(F32)
    vector_sum = jnp.sum(
        got[:, :rows_v].reshape(y_count, win_count, rows_v, width), axis=1
    ).astype(BF16)
    weight_sum = jnp.sum(got[:, rows_v:], axis=0).astype(BF16)
    got = exchange(
        jnp.broadcast_to(weight_sum[None], (inner_count, rows_v, width)),
        axis_index_groups=inner_groups,
    ).astype(F32)
    weight_sum = jnp.sum(got, axis=0).astype(BF16)
    back = jnp.concatenate(
        [
            jnp.broadcast_to(
                vector_sum[:, None], (y_count, win_count, rows_v, width)
            ).reshape(groups, rows_v, width),
            jnp.broadcast_to(weight_sum[None], (groups, rows_v, width)),
        ],
        axis=1,
    )
    got = exchange(back, axis_index_groups=outer_groups).astype(F32)
    vector_grad = got[:, :rows_v].reshape(nodes, width)
    weight_grad = got[:, rows_v:].reshape(nodes, width)[: 3 * width].reshape(3, width, width)
    return (out.reshape(features.shape), vector_grad, weight_grad)


def solution(mesh):
    placed = (
        P("node", "win", None, None),
        P("node", None),
        P(),
        P(),
        P(),
        P("node", "win", None, None),
    )
    return jax.shard_map(
        body,
        mesh=mesh,
        in_specs=placed,
        out_specs=(P("node", "win", None, None), P("node", None), P()),
        check_vma=False,
    )
```

time: 481 us -> 87.3 us (0.18)
  waiting for transfers between devices: 393 us -> 11.9 us
  blocking collectives: 0 us -> 35.4 us
  matrix products: 29.5 us -> 0 us
  between operations: 14.6 us -> 0.75 us
  Pallas kernels: 0 us -> 8.52 us
  starting transfers between devices: 29 us -> 23.1 us
    psum x2 -> x0, waiting for transfers between devices: 387 us -> none  [the longest x1 274 us: body(): weight_grad = lax.psum(partial_mix, ('node', 'win'))]
    all_to_all x0 -> x2, blocking collectives: none -> 35.4 us  [the longest x1 20.1 us: body(): got = exchange(sums, axis_index_groups=outer_groups).astype(F32)]
    dot_general x19 -> x0, matrix products: 29.5 us -> none  [the longest x2 4.96 us: dense_product(): return jnp.dot(adj_rounded, wide_rows, preferred_element_type=jnp.float32)]
    ppermute x8 -> x2, starting transfers between devices: 29 us -> 10.1 us  [the longest x1 5.38 us: body(): lax.ppermute(tail, 'node', [(i, i + 1) for i in range(node_count - 1)])]
    all_to_all x0 -> x1, starting transfers between devices: none -> 13 us  [body(): exchange(jnp.broadcast_to(weight_sum[None], (inner_count, rows_v, width))...]
    pallas_call x0 -> x2, Pallas kernels: none -> 8.52 us  [the longest x1 7.96 us: body(): pl.pallas_call(partial(layer_kernel, 1.0 / math.sqrt(flat * node_count *...]
    all_to_all x0 -> x1, waiting for transfers between devices: none -> 7.75 us  [body(): exchange(jnp.broadcast_to(weight_sum[None], (inner_count, rows_v, width))...]
  transfers between devices with their start and end apart: 10 -> 3, of which waited for: 6 -> 2; matrix products, arithmetic and copies ran while one was open for 3% -> 1% of each run, Pallas kernels for 0% -> 0%
where the time goes in v1:
time: 87.3 us; the launch traced here: 86.9 us
  blocking collectives  35.4 us (41%)
  starting transfers between devices  23.1 us (26%)
  waiting for transfers between devices  11.9 us (14%)
  Pallas kernels  8.52 us (10%)
  local copies, waits for them, and re-layouts  6.54 us (7%)
    all_to_all x1, blocking collectives, body(): got = exchange(sums, axis_index_groups=outer_groups).astype(F32)  20.1 us
    all_to_all x1, blocking collectives, body(): got = exchange(back, axis_index_groups=outer_groups).astype(F32)  15.3 us
    all_to_all x1, starting transfers between devices, body(): exchange(jnp.broadcast_to(weight_sum[None], (inner_count, rows_v, width))...  13 us
    pallas_call x1, Pallas kernels, body(): pl.pallas_call(partial(layer_kernel, 1.0 / math.sqrt(flat * node_count *...  7.96 us
    all_to_all x1, waiting for transfers between devices, body(): exchange(jnp.broadcast_to(weight_sum[None], (inner_count, rows_v, width))...  7.75 us
    ppermute x1, starting transfers between devices, body(): lax.ppermute(tail, 'node', [(i, i + 1) for i in range(node_count - 1)])  5.38 us
    ppermute x1, starting transfers between devices, body(): lax.ppermute(head, 'node', [(i + 1, i) for i in range(node_count - 1)])  4.69 us
    unnamed x14, local copies, waits for them, and re-layouts  4.34 us
  transfers between devices with their start and end apart: 3, of which 2 were waited for; matrix products, arithmetic and copies ran while one was open for 1% of the time, Pallas kernels for 0%

profile of v1, /device:TPU:1, one launch (start us, length us, event | category | flops | bytes accessed | tf_op | source)
XLA Modules:
  0.0 86.9 jit_solution(1451661992350723195)
XLA Ops:
  0.6 0.0 copy-start
  0.6 0.9 %copy-done = bf16[512,1,2,128]{3,2,1,0:T(2,128)(2,1)S(1)} copy-done((bf16[512,1,2,128]{3,2,1,0:T(2,128)(2,1)S(1)}, bf16[512,1,2,128]{3,2,1,0:T(2,128)(2,1)}, u32[]{:S(2)}) %copy-start) | copy-done | bytes 262168
  1.6 0.0 copy-start.1
  1.6 0.9 %copy-done.1 = bf16[512,1,2,128]{3,2,1,0:T(2,128)(2,1)S(1)} copy-done((bf16[512,1,2,128]{3,2,1,0:T(2,128)(2,1)S(1)}, bf16[512,1,2,128]{3,2,1,0:T(2,128)(2,1)}, u32[]{:S(2)}) %copy-start.1) | copy-done | bytes 262168
  2.5 0.0 copy-start.2
  2.5 0.9 %copy-done.2 = f32[512,128]{1,0:T(8,128)S(1)} copy-done((f32[512,128]{1,0:T(8,128)S(1)}, f32[512,128]{1,0:T(8,128)}, u32[]{:S(2)}) %copy-start.2) | copy-done | bytes 262168
  3.5 0.0 copy-start.3
  3.5 0.8 copy-done.3
  4.3 0.6 pack.1
  4.9 5.4 %collective-permute-start = (bf16[384,640]{1,0:T(8,128)(2,1)S(1)}, bf16[384,640]{1,0:T(8,128)(2,1)S(1)}, u32[]{:S(2)}, u32[]{:S(2)}) collective-permute-start(bf16[384,640]{1,0:T(8,128)(2,1)S(1)} %get-tuple-element.8.tail_ref), channel_id=1, source_target_pairs={{0,8},{8,16},{16,24},{24,32},{32,40},{40,48},{48,56},{56,64},{64,7... | collective-permute-start | bytes 1474568 | tf_op jit(solution)/shard_map/ppermute | solution.py:317
  10.3 4.7 %collective-permute-start.1 = (bf16[384,640]{1,0:T(8,128)(2,1)S(1)}, bf16[384,640]{1,0:T(8,128)(2,1)S(1)}, u32[]{:S(2)}, u32[]{:S(2)}) collective-permute-start(bf16[384,640]{1,0:T(8,128)(2,1)S(1)} %get-tuple-element.9.head_ref), channel_id=1, source_target_pairs={{8,0},{16,8},{24,16},{32,24},{40,32},{48,40},{56,48},{64,56},{72,6... | collective-permute-start | bytes 1474568 | tf_op jit(solution)/shard_map/ppermute | solution.py:318
  15.0 0.0 copy-start.6
  15.0 0.6 copy-done.6
  15.6 0.1 copy.13
  15.8 0.0 copy-start.5
  15.8 0.2 reduce-window.8
  15.9 0.0 copy-start.4
  15.9 0.1 reduce.1
  16.1 0.2 convert_reduce_fusion
  16.2 0.0 collective-permute-done.low_ref
  16.3 4.2 %collective-permute-done.1.high_ref = bf16[384,640]{1,0:T(8,128)(2,1)S(1)} collective-permute-done((bf16[384,640]{1,0:T(8,128)(2,1)S(1)}, bf16[384,640]{1,0:T(8,128)(2,1)S(1)}, u32[]{:S(2)}, u32[]{:S(2)}) %collective-permute-start.1) | collective-permute-done | bytes 491552 | tf_op jit(solution)/shard_map/ppermute | solution.py:318
  20.4 0.0 copy-done.5
  20.4 0.0 copy-done.4
  20.4 8.0 %layer.1 = (bf16[1024,128]{1,0:T(8,128)(2,1)}, bf16[32,32,128]{2,1,0:T(8,128)(2,1)S(1)}) custom-call(s32[10]{0:T(128)S(1)} %and_select_fusion.region_ref, bf16[384,640]{1,0:T(8,128)(2,1)S(1)} %collective-permute-done.low_ref, bf16[384,640]{1,0:T(8,128)(2,1)S(1)} %collective-permute-done.1.high_ref, bf16[384,640]{1,0:T(8,128)(2,1)S(1)} %get-tuple-element.9.head_ref, ...), custom_call_target="tpu_custom_call" | custom-call | tf_op jit(solution)/shard_map/layer/pallas_call | solution.py:332
  28.4 20.1 %all_to_all.15 = bf16[32,32,128]{2,1,0:T(8,128)(2,1)S(1)} all-to-all(bf16[32,32,128]{2,1,0:T(8,128)(2,1)S(1)} %get-tuple-element.12), channel_id=1, replica_groups={{0,1,2,3,4,5,6,7,128,129,130,131,132,133,134,135,256,257,258,259,260,26..., dimensions={0} | all-to-all | bytes 524288 | tf_op jit(solution)/shard_map/all_to_all | solution.py:366
  48.5 0.1 convert_element_type.26
  48.6 0.6 broadcast_in_dim.12
  49.3 13.0 %all-to-all-start.1 = ((bf16[16,16,128]{2,1,0:T(8,128)(2,1)}), bf16[16,16,128]{2,1,0:T(8,128)(2,1)S(1)}, u32[]{:S(2)}, u32[]{:S(2)}) async-start(bf16[16,16,128]{2,1,0:T(8,128)(2,1)} %broadcast_in_dim.12), calls=%async_computation.1 | async-start | bytes 131072 | tf_op jit(solution)/shard_map/all_to_all | solution.py:371
  62.3 7.8 %all-to-all-done.1 = bf16[16,16,128]{2,1,0:T(8,128)(2,1)S(1)} async-done(((bf16[16,16,128]{2,1,0:T(8,128)(2,1)}), bf16[16,16,128]{2,1,0:T(8,128)(2,1)S(1)}, u32[]{:S(2)}, u32[]{:S(2)}) %all-to-all-start.1) | async-done | bytes 65568 | tf_op jit(solution)/shard_map/all_to_all | solution.py:371
  70.1 15.3 %all_to_all.16 = bf16[32,32,128]{2,1,0:T(8,128)(2,1)S(1)} all-to-all(bf16[32,32,128]{2,1,0:T(8,128)(2,1)S(1)} %pad_maximum_fusion), channel_id=1, replica_groups={{0,1,2,3,4,5,6,7,128,129,130,131,132,133,134,135,256,257,258,259,260,26..., dimensions={0} | all-to-all | bytes 524288 | tf_op jit(solution)/shard_map/all_to_all | solution.py:385
  85.5 0.7 slice.22
  86.2 0.7 slice.21
  (8 shorter events, 0.1 us)
Async XLA Ops:
  0.6 1.0 %copy-start = (bf16[512,1,2,128]{3,2,1,0:T(2,128)(2,1)S(1)}, bf16[512,1,2,128]{3,2,1,0:T(2,128)(2,1)}, u32[]{:S(2)}) copy-start(bf16[512,1,2,128]{3,2,1,0:T(2,128)(2,1)} %param.6) | copy-start | bytes 786436
  1.6 0.9 %copy-start.1 = (bf16[512,1,2,128]{3,2,1,0:T(2,128)(2,1)S(1)}, bf16[512,1,2,128]{3,2,1,0:T(2,128)(2,1)}, u32[]{:S(2)}) copy-start(bf16[512,1,2,128]{3,2,1,0:T(2,128)(2,1)} %param.11) | copy-start | bytes 786436
  2.5 0.9 %copy-start.2 = (f32[512,128]{1,0:T(8,128)S(1)}, f32[512,128]{1,0:T(8,128)}, u32[]{:S(2)}) copy-start(f32[512,128]{1,0:T(8,128)} %nv_ref.1) | copy-start | bytes 786436
  3.5 0.8 copy-start.3
  4.9 11.4 %collective-permute-start = (bf16[384,640]{1,0:T(8,128)(2,1)S(1)}, bf16[384,640]{1,0:T(8,128)(2,1)S(1)}, u32[]{:S(2)}, u32[]{:S(2)}) collective-permute-start(bf16[384,640]{1,0:T(8,128)(2,1)S(1)} %get-tuple-element.8.tail_ref), channel_id=1, source_target_pairs={{0,8},{8,16},{16,24},{24,32},{32,40},{40,48},{48,56},{56,64},{64,7... | collective-permute-start | bytes 1474568 | tf_op jit(solution)/shard_map/ppermute | solution.py:317
  10.3 10.1 %collective-permute-start.1 = (bf16[384,640]{1,0:T(8,128)(2,1)S(1)}, bf16[384,640]{1,0:T(8,128)(2,1)S(1)}, u32[]{:S(2)}, u32[]{:S(2)}) collective-permute-start(bf16[384,640]{1,0:T(8,128)(2,1)S(1)} %get-tuple-element.9.head_ref), channel_id=1, source_target_pairs={{8,0},{16,8},{24,16},{32,24},{40,32},{48,40},{56,48},{64,56},{72,6... | collective-permute-start | bytes 1474568 | tf_op jit(solution)/shard_map/ppermute | solution.py:318
  15.0 0.7 copy-start.6
  15.8 4.7 %copy-start.5 = (bf16[3,128,128]{2,1,0:T(8,128)(2,1)S(1)}, bf16[3,128,128]{2,1,0:T(8,128)(2,1)}, u32[]{:S(2)}) copy-start(bf16[3,128,128]{2,1,0:T(8,128)(2,1)} %mix_ref.1) | copy-start | bytes 294916
  15.9 4.5 %copy-start.4 = (f32[2,64,64]{2,1,0:T(8,128)S(1)}, f32[2,64,64]{2,1,0:T(8,128)}, u32[]{:S(2)}) copy-start(f32[2,64,64]{2,1,0:T(8,128)} %proj_ref.3) | copy-start | bytes 98308
  49.3 20.8 %all-to-all-start.1 = ((bf16[16,16,128]{2,1,0:T(8,128)(2,1)}), bf16[16,16,128]{2,1,0:T(8,128)(2,1)S(1)}, u32[]{:S(2)}, u32[]{:S(2)}) async-start(bf16[16,16,128]{2,1,0:T(8,128)(2,1)} %broadcast_in_dim.12), calls=%async_computation.1 | async-start | bytes 131072 | tf_op jit(solution)/shard_map/all_to_all | solution.py:371

commit v2 on v1

v2 whole, which is shorter than its diff:
```python
from functools import partial
import math

import jax
import jax.numpy as jnp
from jax import lax
from jax.experimental import pallas as pl
from jax.experimental.pallas import tpu as pltpu
from jax.sharding import PartitionSpec as P

BLOCK = 128
HALO = 3
KEEP_INPUT = 0.05
F32 = jnp.float32
BF16 = jnp.bfloat16
NT = (((1,), (1,)), ((), ()))
TN = (((0,), (0,)), ((), ()))
HIGHEST = lax.Precision.HIGHEST


def block_diagonal(projections):
    zero = jnp.zeros_like(projections[0])
    return jnp.concatenate(
        [
            jnp.concatenate([projections[0], zero], axis=1),
            jnp.concatenate([zero, projections[1]], axis=1),
        ],
        axis=0,
    )


def pack_kernel(
    x_hbm, g_hbm, nv_hbm, proj_hbm, own_ref, far_ref, near_ref, m_ref, x_in, g_in, nv_in, proj_in,
    flat_ref, sems,
):
    copies = [
        pltpu.make_async_copy(source, target, sems.at[i])
        for i, (source, target) in enumerate(
            ((x_hbm, x_in), (g_hbm, g_in), (nv_hbm, nv_in), (proj_hbm, proj_in))
        )
    ]
    for copy in copies:
        copy.start()
    nodes, width = m_ref.shape
    rim = far_ref.shape[0]
    for part, source in enumerate((x_in, g_in)):
        copies[part].wait()
        flat_ref[...] = source[...].astype(F32)
        for step in range(2):
            rows = flat_ref[pl.ds(step, nodes, stride=2), :].astype(BF16)
            own_ref[:, (2 * part + step) * width : (2 * part + step + 1) * width] = rows
    copies[2].wait()
    copies[3].wait()
    learned = jnp.tanh(
        3.0
        * jnp.dot(
            nv_in[...],
            block_diagonal(proj_in[...]),
            precision=HIGHEST,
            preferred_element_type=F32,
        )
    )
    m_ref[...] = learned
    own_ref[:, 4 * width :] = learned.astype(BF16)
    odd = lax.rem(lax.axis_index("node"), 2)
    gap = nodes - rim
    far_ref[...] = own_ref[pl.ds(pl.multiple_of(odd * gap, BLOCK), rim), :]
    near_ref[...] = own_ref[pl.ds(pl.multiple_of((1 - odd) * gap, BLOCK), rim), :]


def layer_kernel(
    norm_scale,
    region_ref,
    first_ref,
    far_ref,
    near_ref,
    own_ref,
    m_ref,
    proj_ref,
    mix_ref,
    out_ref,
    sums_ref,
    x_ref,
    g_ref,
    learned_ref,
    swapped_ref,
    adj_ref,
    adjt_ref,
    score_ref,
    rdeg_ref,
    one_ref,
    two_ref,
    q_one_ref,
    q_two_ref,
    off_ref,
    offrow_ref,
    flat_ref,
):
    b = BLOCK
    nodes, width = m_ref.shape
    rim = far_ref.shape[0]
    own_units = nodes // b
    units = own_units + 2 * HALO
    reach = HALO + 1
    row = 2 * width
    odd = lax.rem(lax.axis_index("node"), 2)
    span = rim + nodes
    pieces = (
        (pl.multiple_of(odd * span, b), far_ref, rim),
        (rim, own_ref, nodes),
        (pl.multiple_of((1 - odd) * span, b), near_ref, rim),
    )
    for start, source, count in pieces:
        place = pl.ds(start, count)
        x_ref[place, :] = source[:, :row]
        g_ref[place, :] = source[:, row : 2 * row]
        learned_ref[place, :] = source[:, 2 * row :]
    learned = learned_ref[...]
    half = width // 2
    swapped_ref[...] = jnp.concatenate([learned[:, half:], -learned[:, :half]], axis=1)

    def unit_rows(first, count=1):
        return slice(first * b, (first + count) * b)

    firsts = [first_ref[u] for u in range(units)]
    windows = [pl.ds(pl.multiple_of(firsts[u] * b, b), reach * b) for u in range(units)]
    eye = (
        lax.broadcasted_iota(jnp.int32, (b, b), 0) == lax.broadcasted_iota(jnp.int32, (b, b), 1)
    ).astype(F32)
    own_first = HALO
    own_last = own_first + own_units
    for u in range(units):
        rows = unit_rows(u)
        scores = lax.dot_general(
            learned_ref[rows, :], swapped_ref[windows[u], :], NT, preferred_element_type=F32
        )
        mine = region_ref[u]
        mask = jnp.concatenate(
            [
                jnp.full(
                    (1, b),
                    jnp.where((region_ref[firsts[u] + k] == mine) & (mine >= 0), 1.0, 0.0),
                    F32,
                )
                for k in range(reach)
            ],
            axis=1,
        )
        squashed = jnp.tanh(3.0 * scores) * mask
        if own_first <= u < own_last:
            score_ref[unit_rows(u - own_first), :] = squashed
        positive = jnp.maximum(squashed, 0.0)
        negative = jnp.minimum(squashed, 0.0)
        forward = positive * positive
        adj_ref[rows, :] = forward.astype(BF16)
        adjt_ref[rows, :] = (negative * negative).astype(BF16)
        diagonal = pl.ds(pl.multiple_of((u - firsts[u]) * b, b), b)
        adj_ref[rows, diagonal] = (adj_ref[rows, diagonal].astype(F32) + eye).astype(BF16)
        adjt_ref[rows, diagonal] = (adjt_ref[rows, diagonal].astype(F32) + eye).astype(BF16)
        degree = 1.0 + jnp.sum(forward, axis=1, keepdims=True)
        rdeg_ref[rows, :] = jnp.broadcast_to(1.0 / degree, (b, width))

    def twice(values):
        return jnp.concatenate([values, values], axis=1)

    def per_step(rows, weight, dims):
        return jnp.concatenate(
            [
                lax.dot_general(
                    rows[:, s * width : (s + 1) * width], weight, dims, preferred_element_type=F32
                )
                for s in range(2)
            ],
            axis=1,
        )

    keep = 1.0 - KEEP_INPUT
    for r in range(0, units, 2):
        rows = unit_rows(r, 2)
        back_two = per_step(g_ref[rows, :], mix_ref[2], NT)
        q_two_ref[rows, :] = (keep * back_two * twice(rdeg_ref[rows, :])).astype(BF16)
    for u in range(units):
        rows = unit_rows(u)
        rdeg = twice(rdeg_ref[rows, :])
        carried = jnp.dot(
            adjt_ref[rows, :], q_two_ref[windows[u], :], preferred_element_type=F32
        )
        back_one = per_step(g_ref[rows, :], mix_ref[1], NT) + carried
        grad_one = (keep * back_one * rdeg).astype(BF16)
        q_one_ref[rows, :] = grad_one
        prop = jnp.dot(adj_ref[rows, :], x_ref[windows[u], :], preferred_element_type=F32) * rdeg
        one_ref[rows, :] = (KEEP_INPUT * x_ref[rows, :].astype(F32) + keep * prop).astype(BF16)
        off_ref[rows, :] = jnp.broadcast_to(
            jnp.sum(grad_one.astype(F32) * prop, axis=1, keepdims=True), (b, width)
        )
    for u in range(units):
        rows = unit_rows(u)
        prop = jnp.dot(
            adj_ref[rows, :], one_ref[windows[u], :], preferred_element_type=F32
        ) * twice(rdeg_ref[rows, :])
        offset = off_ref[rows, :] + jnp.broadcast_to(
            jnp.sum(q_two_ref[rows, :].astype(F32) * prop, axis=1, keepdims=True), (b, width)
        )
        off_ref[rows, :] = offset
        offrow_ref[u] = jnp.transpose(offset)[:8]
        if own_first <= u < own_last:
            two_ref[unit_rows(u - own_first), :] = (
                KEEP_INPUT * x_ref[rows, :].astype(F32) + keep * prop
            ).astype(BF16)

    own = unit_rows(own_first, own_units)
    hops = (x_ref[own, :], one_ref[own, :], two_ref[...])
    plain = (((1,), (0,)), ((), ()))
    mixed = per_step(hops[0], mix_ref[0], plain)
    for k in (1, 2):
        mixed = mixed + per_step(hops[k], mix_ref[k], plain)
    for s in range(2):
        flat_ref[pl.ds(s, nodes, stride=2), :] = mixed[:, s * width : (s + 1) * width]
    out_ref[...] = flat_ref[...].astype(BF16)

    groups = sums_ref.shape[0]
    rows_v = nodes // groups
    weight_rows = []
    for hop in hops:
        total = jnp.zeros((width, width), F32)
        for s in range(2):
            cut = slice(s * width, (s + 1) * width)
            total = total + lax.dot_general(
                hop[:, cut], g_ref[own, cut], TN, preferred_element_type=F32
            )
        weight_rows.append((total * norm_scale).astype(BF16))
    weight_rows.append(jnp.zeros((groups * rows_v - 3 * width, width), BF16))
    weights = jnp.concatenate(weight_rows, axis=0)
    for k in range(groups):
        sums_ref[k, rows_v:, :] = weights[k * rows_v : (k + 1) * rows_v]

    diagonal = block_diagonal(proj_ref[...])
    for u in range(own_first, own_last):
        rows = unit_rows(u)
        columns = windows[u]
        inner = lax.dot_general(
            q_one_ref[rows, :], x_ref[columns, :], NT, preferred_element_type=F32
        ) + lax.dot_general(
            q_two_ref[rows, :], one_ref[columns, :], NT, preferred_element_type=F32
        )
        inner_t = lax.dot_general(
            x_ref[rows, :], q_one_ref[columns, :], NT, preferred_element_type=F32
        ) + lax.dot_general(
            one_ref[rows, :], q_two_ref[columns, :], NT, preferred_element_type=F32
        )
        local = unit_rows(u - own_first)
        squashed = score_ref[local, :]
        offset = jnp.concatenate([off_ref[rows, :]] * reach, axis=1)
        offset_t = jnp.concatenate(
            [offrow_ref[firsts[u] + k, 0:1, :] for k in range(reach)], axis=1
        )
        chosen = jnp.where(squashed > 0.0, inner - offset, inner_t - offset_t)
        pair = (6.0 * squashed * (1.0 - squashed * squashed) * chosen).astype(BF16)
        grad_m = jnp.dot(pair, swapped_ref[columns, :], preferred_element_type=F32)
        mine = m_ref[local, :]
        grad = lax.dot_general(
            3.0 * (1.0 - mine * mine) * grad_m,
            diagonal,
            NT,
            precision=HIGHEST,
            preferred_element_type=F32,
        ).astype(BF16)
        per = b // rows_v
        for j in range(per):
            sums_ref[(u - own_first) * per + j, :rows_v, :] = grad[j * rows_v : (j + 1) * rows_v]


def finish_kernel(got_ref, vector_ref, weight_ref):
    groups, rows = got_ref.shape[:2]
    half = rows // 2
    for k in range(groups):
        got = got_ref[k].astype(F32)
        vector_ref[k * half : (k + 1) * half, :] = got[:half]
        if (k + 1) * half <= weight_ref.shape[0]:
            weight_ref[k * half : (k + 1) * half, :] = got[half:]


def device_groups(counts, kept):
    strides = [math.prod(counts[i + 1 :]) for i in range(len(counts))]

    def spread(axes):
        numbers = [0]
        for i in axes:
            numbers = [n + k * strides[i] for n in numbers for k in range(counts[i])]
        return numbers

    others = [i for i in range(len(counts)) if i not in kept]
    return [[base + k for k in spread(kept)] for base in spread(others)]


def body(features, node_vectors, projections, mix_weight, region_sizes, cotangent):
    nodes, _, steps, width = features.shape
    axes = ("node", "win")
    node_count, win_count = lax.axis_size("node"), lax.axis_size("win")
    own_units = nodes // BLOCK
    units = own_units + 2 * HALO
    rim = HALO * BLOCK
    flat = nodes * steps
    row = steps * width
    in_vmem = pl.BlockSpec(memory_space=pltpu.VMEM)
    in_hbm = pl.BlockSpec(memory_space=pltpu.HBM)
    own, far, near, learned = pl.pallas_call(
        pack_kernel,
        name="pack",
        in_specs=[in_hbm] * 4,
        out_shape=(
            jax.ShapeDtypeStruct((nodes, 5 * width), BF16),
            jax.ShapeDtypeStruct((rim, 5 * width), BF16),
            jax.ShapeDtypeStruct((rim, 5 * width), BF16),
            jax.ShapeDtypeStruct((nodes, width), F32),
        ),
        scratch_shapes=[
            pltpu.VMEM((flat, width), BF16),
            pltpu.VMEM((flat, width), BF16),
            pltpu.VMEM((nodes, width), F32),
            pltpu.VMEM(projections.shape, F32),
            pltpu.VMEM((flat, width), F32),
            pltpu.SemaphoreType.DMA((4,)),
        ],
        compiler_params=pltpu.CompilerParams(vmem_limit_bytes=16 << 20),
    )(
        features.reshape(flat, width),
        cotangent.reshape(flat, width),
        node_vectors,
        projections,
    )
    border = [(i, i + 1) for i in range(1, node_count - 1, 2)]
    inside = [(i, i + 1) for i in range(0, node_count, 2)]
    far = lax.ppermute(far, "node", border + [(j, i) for i, j in border])
    near = lax.ppermute(near, "node", inside + [(j, i) for i, j in inside])
    lead = lax.axis_index("node") * own_units - HALO
    place = jnp.arange(units, dtype=jnp.int32)
    unit = lead + place
    ends = jnp.cumsum(region_sizes)
    passed = (ends[None, :] <= unit[:, None]).astype(jnp.int32)
    in_range = (unit >= 0) & (unit < node_count * own_units)
    region = jnp.where(in_range, jnp.sum(passed, axis=1), -1)
    first = jnp.sum(passed * region_sizes[None, :], axis=1) - lead
    first = jnp.clip(
        first, jnp.maximum(place - HALO, 0), jnp.minimum(place, units - HALO - 1)
    )

    span = units * BLOCK
    y_count, x_count = 4, win_count
    inner_count = node_count // y_count
    groups = y_count * x_count
    rows_v = nodes // groups
    reach = (HALO + 1) * BLOCK
    out, sums = pl.pallas_call(
        partial(layer_kernel, 1.0 / math.sqrt(flat * node_count * win_count)),
        name="layer",
        in_specs=[pl.BlockSpec(memory_space=pltpu.SMEM)] * 2 + [in_vmem] * 6,
        out_shape=(
            jax.ShapeDtypeStruct((flat, width), BF16),
            jax.ShapeDtypeStruct((groups, 2 * rows_v, width), BF16),
        ),
        scratch_shapes=[
            pltpu.VMEM((span, row), BF16),
            pltpu.VMEM((span, row), BF16),
            pltpu.VMEM((span, width), BF16),
            pltpu.VMEM((span, width), BF16),
            pltpu.VMEM((span, reach), BF16),
            pltpu.VMEM((span, reach), BF16),
            pltpu.VMEM((nodes, reach), F32),
            pltpu.VMEM((span, width), F32),
            pltpu.VMEM((span, row), BF16),
            pltpu.VMEM((nodes, row), BF16),
            pltpu.VMEM((span, row), BF16),
            pltpu.VMEM((span, row), BF16),
            pltpu.VMEM((span, width), F32),
            pltpu.VMEM((units, 8, width), F32),
            pltpu.VMEM((flat, width), F32),
        ],
        compiler_params=pltpu.CompilerParams(vmem_limit_bytes=32 << 20),
    )(region, first, far, near, own, learned, projections, mix_weight)

    counts = (y_count, inner_count, win_count)
    outer_groups = device_groups(counts, (0, 2))
    inner_groups = device_groups(counts, (1,))
    exchange = partial(
        lax.all_to_all, axis_name=axes, split_axis=0, concat_axis=0, tiled=True
    )
    got = exchange(sums, axis_index_groups=outer_groups).astype(F32)
    vector_sum = jnp.sum(
        got[:, :rows_v].reshape(y_count, win_count, rows_v, width), axis=1
    ).astype(BF16)
    weight_sum = jnp.sum(got[:, rows_v:], axis=0).astype(BF16)
    got = exchange(
        jnp.broadcast_to(weight_sum[None], (inner_count, rows_v, width)),
        axis_index_groups=inner_groups,
    ).astype(F32)
    weight_sum = jnp.sum(got, axis=0).astype(BF16)
    back = jnp.concatenate(
        [
            jnp.broadcast_to(
                vector_sum[:, None], (y_count, win_count, rows_v, width)
            ).reshape(groups, rows_v, width),
            jnp.broadcast_to(weight_sum[None], (groups, rows_v, width)),
        ],
        axis=1,
    )
    got = exchange(back, axis_index_groups=outer_groups)
    vector_grad, weight_grad = pl.pallas_call(
        finish_kernel,
        name="finish",
        in_specs=[in_vmem],
        out_shape=(
            jax.ShapeDtypeStruct((nodes, width), F32),
            jax.ShapeDtypeStruct((3 * width, width), F32),
        ),
        compiler_params=pltpu.CompilerParams(vmem_limit_bytes=8 << 20),
    )(got)
    weight_grad = weight_grad.reshape(3, width, width)
    return (out.reshape(features.shape), vector_grad, weight_grad)


def solution(mesh):
    placed = (
        P("node", "win", None, None),
        P("node", None),
        P(),
        P(),
        P(),
        P("node", "win", None, None),
    )
    return jax.shard_map(
        body,
        mesh=mesh,
        in_specs=placed,
        out_specs=(P("node", "win", None, None), P("node", None), P()),
        check_vma=False,
    )
```

time: 87.3 us -> 84.7 us (0.970)
  blocking collectives: 35.4 us -> 39.6 us
  starting transfers between devices: 23.1 us -> 19.5 us
  waiting for transfers between devices: 11.9 us -> 8.91 us
  local copies, waits for them, and re-layouts: 6.54 us -> 5.13 us
  Pallas kernels: 8.52 us -> 9.71 us
    all_to_all x1, blocking collectives: 20.1 us -> 23.9 us  [body(): got = exchange(sums, axis_index_groups=outer_groups).astype(F32)]
    ppermute x2, waiting for transfers between devices: 4.17 us -> 1.16 us  [the longest x1 1.16 us: body(): far = lax.ppermute(far, 'node', border + [(j, i) for i, j in border])]
    all_to_all x1, starting transfers between devices: 13 us -> 10.1 us  [body(): exchange(jnp.broadcast_to(weight_sum[None], (inner_count, rows_v, width))...]
    slice x2 -> x0, local copies, waits for them, and re-layouts: 1.41 us -> none  [the longest x1 0.72 us: body(): vector_grad = got[:, :rows_v].reshape(nodes, width)]
    pallas_call x1 -> x2, Pallas kernels: 0.56 us -> 1.61 us  [the longest x1 0.81 us: body(): pl.pallas_call(pack_kernel, name='pack', in_specs=[in_hbm] * 4, out_shape...]
where the time goes in v2:
time: 84.7 us; the launch traced here: 84.2 us
  blocking collectives  39.6 us (47%)
  starting transfers between devices  19.5 us (23%)
  Pallas kernels  9.71 us (11%)
  waiting for transfers between devices  8.91 us (11%)
  local copies, waits for them, and re-layouts  5.13 us (6%)
    all_to_all x1, blocking collectives, body(): got = exchange(sums, axis_index_groups=outer_groups).astype(F32)  23.9 us
    all_to_all x1, blocking collectives, body(): got = exchange(back, axis_index_groups=outer_groups)  15.7 us
    all_to_all x1, starting transfers between devices, body(): exchange(jnp.broadcast_to(weight_sum[None], (inner_count, rows_v, width))...  10.1 us
    pallas_call x1, Pallas kernels, body(): pl.pallas_call(partial(layer_kernel, 1.0 / math.sqrt(flat * node_count *...  8.1 us
    all_to_all x1, waiting for transfers between devices, body(): exchange(jnp.broadcast_to(weight_sum[None], (inner_count, rows_v, width))...  7.75 us
    ppermute x1, starting transfers between devices, body(): far = lax.ppermute(far, 'node', border + [(j, i) for i, j in border])  5.37 us
    unnamed x14, local copies, waits for them, and re-layouts  4.34 us
    ppermute x1, starting transfers between devices, body(): near = lax.ppermute(near, 'node', inside + [(j, i) for i, j in inside])  4.06 us
  transfers between devices with their start and end apart: 3, of which 2 were waited for; matrix products, arithmetic and copies ran while one was open for 1% of the time, Pallas kernels for 0%

profile of v2, /device:TPU:1, one launch (start us, length us, event | category | flops | bytes accessed | tf_op | source)
XLA Modules:
  0.0 84.2 jit_solution(15429437066006156758)
XLA Ops:
  0.6 0.0 copy-start
  0.6 0.9 %copy-done = bf16[512,1,2,128]{3,2,1,0:T(2,128)(2,1)S(1)} copy-done((bf16[512,1,2,128]{3,2,1,0:T(2,128)(2,1)S(1)}, bf16[512,1,2,128]{3,2,1,0:T(2,128)(2,1)}, u32[]{:S(2)}) %copy-start) | copy-done | bytes 262168
  1.6 0.0 copy-start.1
  1.6 0.9 %copy-done.1 = bf16[512,1,2,128]{3,2,1,0:T(2,128)(2,1)S(1)} copy-done((bf16[512,1,2,128]{3,2,1,0:T(2,128)(2,1)S(1)}, bf16[512,1,2,128]{3,2,1,0:T(2,128)(2,1)}, u32[]{:S(2)}) %copy-start.1) | copy-done | bytes 262168
  2.5 0.0 copy-start.2
  2.5 0.9 %copy-done.2 = f32[512,128]{1,0:T(8,128)S(1)} copy-done((f32[512,128]{1,0:T(8,128)S(1)}, f32[512,128]{1,0:T(8,128)}, u32[]{:S(2)}) %copy-start.2) | copy-done | bytes 262168
  3.5 0.0 copy-start.3
  3.5 0.8 copy-done.3
  4.3 0.8 pack.1
  5.1 5.4 %collective-permute-start = (bf16[384,640]{1,0:T(8,128)(2,1)S(1)}, bf16[384,640]{1,0:T(8,128)(2,1)S(1)}, u32[]{:S(2)}, u32[]{:S(2)}) collective-permute-start(bf16[384,640]{1,0:T(8,128)(2,1)S(1)} %get-tuple-element.11), channel_id=1, source_target_pairs={{8,16},{24,32},{40,48},{56,64},{72,80},{88,96},{104,112},{120,128}... | collective-permute-start | bytes 1474568 | tf_op jit(solution)/shard_map/ppermute | solution.py:334
  10.5 4.1 %collective-permute-start.1 = (bf16[384,640]{1,0:T(8,128)(2,1)S(1)}, bf16[384,640]{1,0:T(8,128)(2,1)S(1)}, u32[]{:S(2)}, u32[]{:S(2)}) collective-permute-start(bf16[384,640]{1,0:T(8,128)(2,1)S(1)} %get-tuple-element.12), channel_id=1, source_target_pairs={{0,8},{16,24},{32,40},{48,56},{64,72},{80,88},{96,104},{112,120},{... | collective-permute-start | bytes 1474568 | tf_op jit(solution)/shard_map/ppermute | solution.py:335
  14.6 0.0 copy-start.6
  14.6 0.6 copy-done.6
  15.3 0.1 copy.13
  15.4 0.0 copy-start.5
  15.4 0.2 reduce-window.8
  15.5 0.0 copy-start.4
  15.5 0.1 reduce.1
  15.7 0.2 fusion.1
  15.9 1.2 %collective-permute-done.far_ref = bf16[384,640]{1,0:T(8,128)(2,1)S(1)} collective-permute-done((bf16[384,640]{1,0:T(8,128)(2,1)S(1)}, bf16[384,640]{1,0:T(8,128)(2,1)S(1)}, u32[]{:S(2)}, u32[]{:S(2)}) %collective-permute-start) | collective-permute-done | bytes 491552 | tf_op jit(solution)/shard_map/ppermute | solution.py:334
  17.0 0.0 collective-permute-done.1.near_ref
  17.0 0.0 copy-done.5
  17.0 0.0 copy-done.4
  17.0 8.1 %layer.1 = (bf16[1024,128]{1,0:T(8,128)(2,1)}, bf16[32,32,128]{2,1,0:T(8,128)(2,1)S(1)}) custom-call(s32[10]{0:T(128)S(1)} %get-tuple-element.30.region_ref, s32[10]{0:T(128)S(1)} %get-tuple-element.31.first_ref, bf16[384,640]{1,0:T(8,128)(2,1)S(1)} %collective-permute-done.far_ref, bf16[384,640]{1,0:T(8,128)(2,1)S(1)} %collective-permute-done.1.near_ref, ...), custom_call_target="tpu_custom_call" | custom-call | tf_op jit(solution)/shard_map/layer/pallas_call | solution.py:354
  25.1 23.9 %all_to_all.15 = bf16[32,32,128]{2,1,0:T(8,128)(2,1)S(1)} all-to-all(bf16[32,32,128]{2,1,0:T(8,128)(2,1)S(1)} %get-tuple-element.16), channel_id=1, replica_groups={{0,1,2,3,4,5,6,7,128,129,130,131,132,133,134,135,256,257,258,259,260,26..., dimensions={0} | all-to-all | bytes 524288 | tf_op jit(solution)/shard_map/all_to_all | solution.py:388
  49.1 0.6 broadcast_in_dim.12
  49.7 10.1 %all-to-all-start.1 = ((bf16[16,16,128]{2,1,0:T(8,128)(2,1)}), bf16[16,16,128]{2,1,0:T(8,128)(2,1)S(1)}, u32[]{:S(2)}, u32[]{:S(2)}) async-start(bf16[16,16,128]{2,1,0:T(8,128)(2,1)} %broadcast_in_dim.12), calls=%async_computation.1 | async-start | bytes 131072 | tf_op jit(solution)/shard_map/all_to_all | solution.py:393
  59.9 7.8 %all-to-all-done.1 = bf16[16,16,128]{2,1,0:T(8,128)(2,1)S(1)} async-done(((bf16[16,16,128]{2,1,0:T(8,128)(2,1)}), bf16[16,16,128]{2,1,0:T(8,128)(2,1)S(1)}, u32[]{:S(2)}, u32[]{:S(2)}) %all-to-all-start.1) | async-done | bytes 65568 | tf_op jit(solution)/shard_map/all_to_all | solution.py:393
  67.7 15.7 %all_to_all.16.got_ref = bf16[32,32,128]{2,1,0:T(8,128)(2,1)S(1)} all-to-all(bf16[32,32,128]{2,1,0:T(8,128)(2,1)S(1)} %pad_maximum_fusion), channel_id=1, replica_groups={{0,1,2,3,4,5,6,7,128,129,130,131,132,133,134,135,256,257,258,259,260,26..., dimensions={0} | all-to-all | bytes 524288 | tf_op jit(solution)/shard_map/all_to_all | solution.py:407
  83.4 0.8 finish.1
  (9 shorter events, 0.2 us)
Async XLA Ops:
  0.6 1.0 %copy-start = (bf16[512,1,2,128]{3,2,1,0:T(2,128)(2,1)S(1)}, bf16[512,1,2,128]{3,2,1,0:T(2,128)(2,1)}, u32[]{:S(2)}) copy-start(bf16[512,1,2,128]{3,2,1,0:T(2,128)(2,1)} %param.6) | copy-start | bytes 786436
  1.6 0.9 %copy-start.1 = (bf16[512,1,2,128]{3,2,1,0:T(2,128)(2,1)S(1)}, bf16[512,1,2,128]{3,2,1,0:T(2,128)(2,1)}, u32[]{:S(2)}) copy-start(bf16[512,1,2,128]{3,2,1,0:T(2,128)(2,1)} %param.11) | copy-start | bytes 786436
  2.5 0.9 %copy-start.2 = (f32[512,128]{1,0:T(8,128)S(1)}, f32[512,128]{1,0:T(8,128)}, u32[]{:S(2)}) copy-start(f32[512,128]{1,0:T(8,128)} %nv_hbm.1) | copy-start | bytes 786436
  3.5 0.8 copy-start.3
  5.1 11.9 %collective-permute-start = (bf16[384,640]{1,0:T(8,128)(2,1)S(1)}, bf16[384,640]{1,0:T(8,128)(2,1)S(1)}, u32[]{:S(2)}, u32[]{:S(2)}) collective-permute-start(bf16[384,640]{1,0:T(8,128)(2,1)S(1)} %get-tuple-element.11), channel_id=1, source_target_pairs={{8,16},{24,32},{40,48},{56,64},{72,80},{88,96},{104,112},{120,128}... | collective-permute-start | bytes 1474568 | tf_op jit(solution)/shard_map/ppermute | solution.py:334
  10.5 6.5 %collective-permute-start.1 = (bf16[384,640]{1,0:T(8,128)(2,1)S(1)}, bf16[384,640]{1,0:T(8,128)(2,1)S(1)}, u32[]{:S(2)}, u32[]{:S(2)}) collective-permute-start(bf16[384,640]{1,0:T(8,128)(2,1)S(1)} %get-tuple-element.12), channel_id=1, source_target_pairs={{0,8},{16,24},{32,40},{48,56},{64,72},{80,88},{96,104},{112,120},{... | collective-permute-start | bytes 1474568 | tf_op jit(solution)/shard_map/ppermute | solution.py:335
  14.6 0.7 copy-start.6
  15.4 1.7 %copy-start.5 = (bf16[3,128,128]{2,1,0:T(8,128)(2,1)S(1)}, bf16[3,128,128]{2,1,0:T(8,128)(2,1)}, u32[]{:S(2)}) copy-start(bf16[3,128,128]{2,1,0:T(8,128)(2,1)} %mix_ref.1) | copy-start | bytes 294916
  15.5 1.5 %copy-start.4 = (f32[2,64,64]{2,1,0:T(8,128)S(1)}, f32[2,64,64]{2,1,0:T(8,128)}, u32[]{:S(2)}) copy-start(f32[2,64,64]{2,1,0:T(8,128)} %proj_ref.1) | copy-start | bytes 98308
  49.7 17.9 %all-to-all-start.1 = ((bf16[16,16,128]{2,1,0:T(8,128)(2,1)}), bf16[16,16,128]{2,1,0:T(8,128)(2,1)S(1)}, u32[]{:S(2)}, u32[]{:S(2)}) async-start(bf16[16,16,128]{2,1,0:T(8,128)(2,1)} %broadcast_in_dim.12), calls=%async_computation.1 | async-start | bytes 131072 | tf_op jit(solution)/shard_map/all_to_all | solution.py:393

commit v3 on v2

--- a/solution.py
+++ b/solution.py
@@ -220,6 +220,7 @@
 
     groups = sums_ref.shape[0]
     rows_v = nodes // groups
+    rows_w = 3 * width // groups
     weight_rows = []
     for hop in hops:
         total = jnp.zeros((width, width), F32)
@@ -228,11 +229,10 @@
             total = total + lax.dot_general(
                 hop[:, cut], g_ref[own, cut], TN, preferred_element_type=F32
             )
-        weight_rows.append((total * norm_scale).astype(BF16))
-    weight_rows.append(jnp.zeros((groups * rows_v - 3 * width, width), BF16))
+        weight_rows.append(total * norm_scale)
     weights = jnp.concatenate(weight_rows, axis=0)
     for k in range(groups):
-        sums_ref[k, rows_v:, :] = weights[k * rows_v : (k + 1) * rows_v]
+        sums_ref[k, rows_v:, :] = weights[k * rows_w : (k + 1) * rows_w].astype(BF16)
 
     diagonal = block_diagonal(proj_ref[...])
     for u in range(own_first, own_last):
@@ -271,13 +271,13 @@
 
 
 def finish_kernel(got_ref, vector_ref, weight_ref):
-    groups, rows = got_ref.shape[:2]
-    half = rows // 2
+    groups = got_ref.shape[0]
+    rows_v = vector_ref.shape[0] // groups
+    rows_w = weight_ref.shape[0] // groups
     for k in range(groups):
         got = got_ref[k].astype(F32)
-        vector_ref[k * half : (k + 1) * half, :] = got[:half]
-        if (k + 1) * half <= weight_ref.shape[0]:
-            weight_ref[k * half : (k + 1) * half, :] = got[half:]
+        vector_ref[k * rows_v : (k + 1) * rows_v, :] = got[:rows_v]
+        weight_ref[k * rows_w : (k + 1) * rows_w, :] = got[rows_v:]
 
 
 def device_groups(counts, kept):
@@ -324,10 +324,15 @@
         ],
         compiler_params=pltpu.CompilerParams(vmem_limit_bytes=16 << 20),
     )(
-        features.reshape(flat, width),
-        cotangent.reshape(flat, width),
-        node_vectors,
-        projections,
+        *(
+            pltpu.with_memory_space_constraint(array, pltpu.HBM)
+            for array in (
+                features.reshape(flat, width),
+                cotangent.reshape(flat, width),
+                node_vectors,
+                projections,
+            )
+        )
     )
     border = [(i, i + 1) for i in range(1, node_count - 1, 2)]
     inside = [(i, i + 1) for i in range(0, node_count, 2)]
@@ -346,10 +351,11 @@
     )
 
     span = units * BLOCK
-    y_count, x_count = 4, win_count
-    inner_count = node_count // y_count
-    groups = y_count * x_count
+    y_far, y_near = 2, 2
+    inner_count = node_count // (y_far * y_near)
+    groups = y_far * win_count
     rows_v = nodes // groups
+    rows_w = 3 * width // groups
     reach = (HALO + 1) * BLOCK
     out, sums = pl.pallas_call(
         partial(layer_kernel, 1.0 / math.sqrt(flat * node_count * win_count)),
@@ -357,7 +363,7 @@
         in_specs=[pl.BlockSpec(memory_space=pltpu.SMEM)] * 2 + [in_vmem] * 6,
         out_shape=(
             jax.ShapeDtypeStruct((flat, width), BF16),
-            jax.ShapeDtypeStruct((groups, 2 * rows_v, width), BF16),
+            jax.ShapeDtypeStruct((groups, rows_v + rows_w, width), BF16),
         ),
         scratch_shapes=[
             pltpu.VMEM((span, row), BF16),
@@ -379,28 +385,27 @@
         compiler_params=pltpu.CompilerParams(vmem_limit_bytes=32 << 20),
     )(region, first, far, near, own, learned, projections, mix_weight)
 
-    counts = (y_count, inner_count, win_count)
-    outer_groups = device_groups(counts, (0, 2))
-    inner_groups = device_groups(counts, (1,))
+    counts = (y_far, y_near, inner_count, win_count)
+    outer_groups = device_groups(counts, (0, 3))
+    inner_groups = device_groups(counts, (1, 2))
     exchange = partial(
         lax.all_to_all, axis_name=axes, split_axis=0, concat_axis=0, tiled=True
     )
     got = exchange(sums, axis_index_groups=outer_groups).astype(F32)
     vector_sum = jnp.sum(
-        got[:, :rows_v].reshape(y_count, win_count, rows_v, width), axis=1
+        got[:, :rows_v].reshape(y_far, win_count, rows_v, width), axis=1
     ).astype(BF16)
     weight_sum = jnp.sum(got[:, rows_v:], axis=0).astype(BF16)
-    got = exchange(
-        jnp.broadcast_to(weight_sum[None], (inner_count, rows_v, width)),
-        axis_index_groups=inner_groups,
-    ).astype(F32)
+    shares = jnp.broadcast_to(weight_sum[None], (y_near * inner_count, rows_w, width))
+    vector_sum, shares = lax.optimization_barrier((vector_sum, shares))
+    got = exchange(shares, axis_index_groups=inner_groups).astype(F32)
     weight_sum = jnp.sum(got, axis=0).astype(BF16)
     back = jnp.concatenate(
         [
             jnp.broadcast_to(
-                vector_sum[:, None], (y_count, win_count, rows_v, width)
+                vector_sum[:, None], (y_far, win_count, rows_v, width)
             ).reshape(groups, rows_v, width),
-            jnp.broadcast_to(weight_sum[None], (groups, rows_v, width)),
+            jnp.broadcast_to(weight_sum[None], (groups, rows_w, width)),
         ],
         axis=1,
     )

time: 84.7 us -> 80.8 us (0.954)
  blocking collectives: 39.6 us -> 57.2 us
  starting transfers between devices: 19.5 us -> 9.43 us
  waiting for transfers between devices: 8.91 us -> 1.16 us
  local copies, waits for them, and re-layouts: 5.13 us -> 0.83 us
    all_to_all x0 -> x1, blocking collectives: none -> 19.7 us  [body(): got = exchange(shares, axis_index_groups=inner_groups).astype(F32)]
    all_to_all x1 -> x0, starting transfers between devices: 10.1 us -> none  [body(): exchange(jnp.broadcast_to(weight_sum[None], (inner_count, rows_v, width))...]
    all_to_all x1 -> x0, waiting for transfers between devices: 7.75 us -> none  [body(): exchange(jnp.broadcast_to(weight_sum[None], (inner_count, rows_v, width))...]
    unnamed x14 -> x6, local copies, waits for them, and re-layouts: 4.34 us -> 0.66 us
    all_to_all x1, blocking collectives: 23.9 us -> 22.8 us  [body(): got = exchange(sums, axis_index_groups=outer_groups).astype(F32)]
    all_to_all x1, blocking collectives: 15.7 us -> 14.7 us  [body(): got = exchange(back, axis_index_groups=outer_groups)]
  transfers between devices with their start and end apart: 3 -> 2, of which waited for: 2 -> 1; matrix products, arithmetic and copies ran while one was open for 1% -> 1% of each run, Pallas kernels for 0% -> 0%
where the time goes in v3:
time: 80.8 us; the launch traced here: 80.5 us
  blocking collectives  57.2 us (71%)
  Pallas kernels  10.5 us (13%)
  starting transfers between devices  9.43 us (12%)
  waiting for transfers between devices  1.16 us (1%)
  local copies, waits for them, and re-layouts  0.83 us (1%)
    all_to_all x1, blocking collectives, body(): got = exchange(sums, axis_index_groups=outer_groups).astype(F32)  22.8 us
    all_to_all x1, blocking collectives, body(): got = exchange(shares, axis_index_groups=inner_groups).astype(F32)  19.7 us
    all_to_all x1, blocking collectives, body(): got = exchange(back, axis_index_groups=outer_groups)  14.7 us
    pallas_call x1, Pallas kernels, body(): pl.pallas_call(partial(layer_kernel, 1.0 / math.sqrt(flat * node_count *...  8.09 us
    ppermute x1, starting transfers between devices, body(): far = lax.ppermute(far, 'node', border + [(j, i) for i, j in border])  5.37 us
    ppermute x1, starting transfers between devices, body(): near = lax.ppermute(near, 'node', inside + [(j, i) for i, j in inside])  4.06 us
    pallas_call x1, Pallas kernels, body(): pl.pallas_call(pack_kernel, name='pack', in_specs=[in_hbm] * 4, out_shape...  1.64 us
  transfers between devices with their start and end apart: 2, of which 1 were waited for; matrix products, arithmetic and copies ran while one was open for 1% of the time, Pallas kernels for 0%

profile of v3, /device:TPU:1, one launch (start us, length us, event | category | flops | bytes accessed | tf_op | source)
XLA Modules:
  0.0 80.5 jit_solution(15622518848166226370)
XLA Ops:
  0.6 1.6 %pack.1 = (bf16[512,640]{1,0:T(8,128)(2,1)S(1)}, bf16[384,640]{1,0:T(8,128)(2,1)S(1)}, bf16[384,640]{1,0:T(8,128)(2,1)S(1)}, f32[512,128]{1,0:T(8,128)S(1)}) custom-call(bf16[1024,128]{1,0:T(8,128)(2,1)} %bitcast.11, bf16[1024,128]{1,0:T(8,128)(2,1)} %bitcast.12, f32[512,128]{1,0:T(8,128)} %nv_hbm.1, f32[2,64,64]{2,1,0:T(8,128)} %proj_ref.1), custom_call_target="tpu_custom_call" | custom-call | tf_op jit(solution)/shard_map/pack/pallas_call | solution.py:307
  2.3 5.4 %collective-permute-start = (bf16[384,640]{1,0:T(8,128)(2,1)S(1)}, bf16[384,640]{1,0:T(8,128)(2,1)S(1)}, u32[]{:S(2)}, u32[]{:S(2)}) collective-permute-start(bf16[384,640]{1,0:T(8,128)(2,1)S(1)} %get-tuple-element.13), channel_id=1, source_target_pairs={{8,16},{24,32},{40,48},{56,64},{72,80},{88,96},{104,112},{120,128}... | collective-permute-start | bytes 1474568 | tf_op jit(solution)/shard_map/ppermute | solution.py:339
  7.7 4.1 %collective-permute-start.1 = (bf16[384,640]{1,0:T(8,128)(2,1)S(1)}, bf16[384,640]{1,0:T(8,128)(2,1)S(1)}, u32[]{:S(2)}, u32[]{:S(2)}) collective-permute-start(bf16[384,640]{1,0:T(8,128)(2,1)S(1)} %get-tuple-element.14), channel_id=1, source_target_pairs={{0,8},{16,24},{32,40},{48,56},{64,72},{80,88},{96,104},{112,120},{... | collective-permute-start | bytes 1474568 | tf_op jit(solution)/shard_map/ppermute | solution.py:340
  11.7 0.0 copy-start.2
  11.7 0.6 copy-done.2
  12.4 0.1 copy.13
  12.5 0.0 copy-start.1
  12.5 0.2 reduce-window.8
  12.7 0.0 copy-start
  12.7 0.1 reduce.1
  12.8 0.2 fusion.1
  13.0 1.2 %collective-permute-done.far_ref = bf16[384,640]{1,0:T(8,128)(2,1)S(1)} collective-permute-done((bf16[384,640]{1,0:T(8,128)(2,1)S(1)}, bf16[384,640]{1,0:T(8,128)(2,1)S(1)}, u32[]{:S(2)}, u32[]{:S(2)}) %collective-permute-start) | collective-permute-done | bytes 491552 | tf_op jit(solution)/shard_map/ppermute | solution.py:339
  14.2 0.0 collective-permute-done.1.near_ref
  14.2 0.0 copy-done.1
  14.2 0.0 copy-done
  14.2 8.1 %layer.1 = (bf16[1024,128]{1,0:T(8,128)(2,1)}, bf16[16,56,128]{2,1,0:T(8,128)(2,1)S(1)}) custom-call(s32[10]{0:T(128)S(1)} %get-tuple-element.34.region_ref, s32[10]{0:T(128)S(1)} %get-tuple-element.35.first_ref, bf16[384,640]{1,0:T(8,128)(2,1)S(1)} %collective-permute-done.far_ref, bf16[384,640]{1,0:T(8,128)(2,1)S(1)} %collective-permute-done.1.near_ref, ...), custom_call_target="tpu_custom_call" | custom-call | tf_op jit(solution)/shard_map/layer/pallas_call | solution.py:360
  22.3 22.8 %all_to_all.15 = bf16[16,56,128]{2,1,0:T(8,128)(2,1)S(1)} all-to-all(bf16[16,56,128]{2,1,0:T(8,128)(2,1)S(1)} %get-tuple-element.18), channel_id=1, replica_groups={{0,1,2,3,4,5,6,7,256,257,258,259,260,261,262,263},{8,9,10,11,12,13,14,1..., dimensions={0} | all-to-all | bytes 458752 | tf_op jit(solution)/shard_map/all_to_all | solution.py:394
  45.2 19.7 %all_to_all.16 = bf16[32,24,128]{2,1,0:T(8,128)(2,1)S(1)} all-to-all(bf16[32,24,128]{2,1,0:T(8,128)(2,1)S(1)} %broadcast_in_dim.11), channel_id=1, replica_groups={{0,8,16,24,32,40,48,56,64,72,80,88,96,104,112,120,128,136,144,152,160,1..., dimensions={0} | all-to-all | bytes 393216 | tf_op jit(solution)/shard_map/all_to_all | solution.py:401
  65.0 14.7 %all_to_all.17.got_ref = bf16[16,56,128]{2,1,0:T(8,128)(2,1)S(1)} all-to-all(bf16[16,56,128]{2,1,0:T(8,128)(2,1)S(1)} %pad_maximum_fusion), channel_id=1, replica_groups={{0,1,2,3,4,5,6,7,256,257,258,259,260,261,262,263},{8,9,10,11,12,13,14,1..., dimensions={0} | all-to-all | bytes 458752 | tf_op jit(solution)/shard_map/all_to_all | solution.py:412
  79.7 0.8 finish.1
  (10 shorter events, 0.2 us)
Async XLA Ops:
  2.3 11.9 %collective-permute-start = (bf16[384,640]{1,0:T(8,128)(2,1)S(1)}, bf16[384,640]{1,0:T(8,128)(2,1)S(1)}, u32[]{:S(2)}, u32[]{:S(2)}) collective-permute-start(bf16[384,640]{1,0:T(8,128)(2,1)S(1)} %get-tuple-element.13), channel_id=1, source_target_pairs={{8,16},{24,32},{40,48},{56,64},{72,80},{88,96},{104,112},{120,128}... | collective-permute-start | bytes 1474568 | tf_op jit(solution)/shard_map/ppermute | solution.py:339
  7.7 6.5 %collective-permute-start.1 = (bf16[384,640]{1,0:T(8,128)(2,1)S(1)}, bf16[384,640]{1,0:T(8,128)(2,1)S(1)}, u32[]{:S(2)}, u32[]{:S(2)}) collective-permute-start(bf16[384,640]{1,0:T(8,128)(2,1)S(1)} %get-tuple-element.14), channel_id=1, source_target_pairs={{0,8},{16,24},{32,40},{48,56},{64,72},{80,88},{96,104},{112,120},{... | collective-permute-start | bytes 1474568 | tf_op jit(solution)/shard_map/ppermute | solution.py:340
  11.7 0.7 copy-start.2
  12.5 1.7 %copy-start.1 = (bf16[3,128,128]{2,1,0:T(8,128)(2,1)S(1)}, bf16[3,128,128]{2,1,0:T(8,128)(2,1)}, u32[]{:S(2)}) copy-start(bf16[3,128,128]{2,1,0:T(8,128)(2,1)} %mix_ref.1) | copy-start | bytes 294916
  12.7 1.5 %copy-start = (f32[2,64,64]{2,1,0:T(8,128)S(1)}, f32[2,64,64]{2,1,0:T(8,128)}, u32[]{:S(2)}) copy-start(f32[2,64,64]{2,1,0:T(8,128)} %proj_ref.1) | copy-start | bytes 98308

commit v4 on v3

v4 whole, which is shorter than its diff:
```python
from functools import partial
import math

import jax
import jax.numpy as jnp
from jax import lax
from jax.experimental import pallas as pl
from jax.experimental.pallas import tpu as pltpu
from jax.sharding import PartitionSpec as P


BLOCK = 128
HALO = 3
KEEP_INPUT = 0.05
F32 = jnp.float32
BF16 = jnp.bfloat16
NT = (((1,), (1,)), ((), ()))
TN = (((0,), (0,)), ((), ()))
HIGHEST = lax.Precision.HIGHEST


def block_diagonal(projections):
    zero = jnp.zeros_like(projections[0])
    return jnp.concatenate(
        [
            jnp.concatenate([projections[0], zero], axis=1),
            jnp.concatenate([zero, projections[1]], axis=1),
        ],
        axis=0,
    )


def pack_kernel(
    x_hbm, g_hbm, nv_hbm, proj_hbm, own_ref, far_ref, far_g_ref, near_ref, m_ref, x_in, g_in, nv_in,
    proj_in, flat_ref, sems,
):
    copies = [
        pltpu.make_async_copy(source, target, sems.at[i])
        for i, (source, target) in enumerate(
            ((x_hbm, x_in), (g_hbm, g_in), (nv_hbm, nv_in), (proj_hbm, proj_in))
        )
    ]
    for copy in copies:
        copy.start()
    nodes, width = m_ref.shape
    rim = far_ref.shape[0]
    for part, source in enumerate((x_in, g_in)):
        copies[part].wait()
        flat_ref[...] = source[...].astype(F32)
        for step in range(2):
            rows = flat_ref[pl.ds(step, nodes, stride=2), :].astype(BF16)
            first = (1 + 2 * part + step) * width
            own_ref[:, first : first + width] = rows
    copies[2].wait()
    copies[3].wait()
    learned = jnp.tanh(
        3.0
        * jnp.dot(
            nv_in[...],
            block_diagonal(proj_in[...]),
            precision=HIGHEST,
            preferred_element_type=F32,
        )
    )
    m_ref[...] = learned
    own_ref[:, :width] = learned.astype(BF16)
    odd = lax.rem(lax.axis_index("node"), 2)
    gap = nodes - rim
    far_rows = pl.ds(pl.multiple_of(odd * gap, BLOCK), rim)
    far_ref[...] = own_ref[far_rows, : 3 * width]
    far_g_ref[...] = own_ref[far_rows, 3 * width :]
    near_ref[...] = own_ref[pl.ds(pl.multiple_of((1 - odd) * gap, BLOCK), rim), :]


def unit_rows(first, count=1):
    return slice(first * BLOCK, (first + count) * BLOCK)


def rim_places(rim, nodes):
    odd = lax.rem(lax.axis_index("node"), 2)
    span = rim + nodes
    return (
        pl.ds(pl.multiple_of(odd * span, BLOCK), rim),
        pl.ds(pl.multiple_of((1 - odd) * span, BLOCK), rim),
    )


def twice(values):
    return jnp.concatenate([values, values], axis=1)


def forward_kernel(
    norm_scale,
    region_ref,
    first_ref,
    far_ref,
    near_ref,
    own_ref,
    mix_hbm,
    out_ref,
    sums_ref,
    swapped_ref,
    hops_ref,
    props_ref,
    adjt_ref,
    score_ref,
    rdeg_ref,
    learned_ref,
    adj_ref,
    two_ref,
    flat_ref,
    mix_ref,
    sem,
):
    mix_copy = pltpu.make_async_copy(mix_hbm, mix_ref, sem)
    mix_copy.start()
    b = BLOCK
    nodes = own_ref.shape[0]
    rim, width = far_ref.shape[0], far_ref.shape[1] // 3
    own_units = nodes // b
    units = own_units + 2 * HALO
    reach = HALO + 1
    row = 2 * width
    half = width // 2
    far_place, near_place = rim_places(rim, nodes)
    own_place = pl.ds(rim, nodes)
    for place, source in ((far_place, far_ref), (own_place, own_ref), (near_place, near_ref)):
        learned = source[:, :width]
        learned_ref[place, :] = learned
        swapped_ref[place, :] = jnp.concatenate(
            [learned[:, half:], -learned[:, :half]], axis=1
        )
        hops_ref[place, :row] = source[:, width : 3 * width]

    firsts = [first_ref[u] for u in range(units)]
    eye = (
        lax.broadcasted_iota(jnp.int32, (b, b), 0) == lax.broadcasted_iota(jnp.int32, (b, b), 1)
    ).astype(F32)
    own_first = HALO
    own_last = own_first + own_units
    for u in range(units):
        rows = unit_rows(u)
        mine = region_ref[u]
        total = jnp.zeros((b, b), F32)
        for k in range(reach):
            other = firsts[u] + k
            scores = lax.dot_general(
                learned_ref[rows, :],
                swapped_ref[pl.ds(pl.multiple_of(other * b, b), b), :],
                NT,
                preferred_element_type=F32,
            )
            same = jnp.where((region_ref[other] == mine) & (mine >= 0), 1.0, 0.0)
            squashed = jnp.tanh(3.0 * scores) * same
            positive = jnp.maximum(squashed, 0.0)
            negative = jnp.minimum(squashed, 0.0)
            forward = positive * positive
            columns = unit_rows(k)
            if own_first <= u < own_last:
                score_ref[unit_rows(u - own_first), columns] = squashed
            adj_ref[rows, columns] = forward.astype(BF16)
            adjt_ref[rows, columns] = (negative * negative).astype(BF16)
            total = total + forward
        diagonal = pl.ds(pl.multiple_of((u - firsts[u]) * b, b), b)
        adj_ref[rows, diagonal] = (adj_ref[rows, diagonal].astype(F32) + eye).astype(BF16)
        adjt_ref[rows, diagonal] = (adjt_ref[rows, diagonal].astype(F32) + eye).astype(BF16)
        degree = 1.0 + jnp.sum(total, axis=1, keepdims=True)
        rdeg_ref[rows, :] = jnp.broadcast_to(1.0 / degree, (b, width))

    keep = 1.0 - KEEP_INPUT
    windows = [pl.ds(pl.multiple_of(firsts[u] * b, b), reach * b) for u in range(units)]
    for hop in range(2):
        source = slice(hop * row, (hop + 1) * row)
        for u in range(units):
            rows = unit_rows(u)
            prop = jnp.dot(
                adj_ref[rows, :], hops_ref[windows[u], source], preferred_element_type=F32
            ) * twice(rdeg_ref[rows, :])
            props_ref[rows, source] = prop.astype(BF16)
            if hop == 0:
                hops_ref[rows, row:] = (
                    KEEP_INPUT * hops_ref[rows, :row].astype(F32) + keep * prop
                ).astype(BF16)
            elif own_first <= u < own_last:
                two_ref[unit_rows(u - own_first), :] = (
                    KEEP_INPUT * hops_ref[rows, :row].astype(F32) + keep * prop
                ).astype(BF16)

    mix_copy.wait()
    weights = jnp.concatenate([mix_ref[0], mix_ref[1], mix_ref[2]], axis=0)
    all_hops, all_up = [], []
    for s in range(2):
        cut = slice(s * width, (s + 1) * width)
        all_hops.append(
            jnp.concatenate(
                [
                    hops_ref[own_place, cut],
                    hops_ref[own_place, row + s * width : row + (s + 1) * width],
                    two_ref[:, cut],
                ],
                axis=1,
            )
        )
        all_up.append(own_ref[:, 3 * width + s * width : 3 * width + (s + 1) * width])
        flat_ref[pl.ds(s, nodes, stride=2), :] = jnp.dot(
            all_hops[s], weights, preferred_element_type=F32
        )
    out_ref[...] = flat_ref[...].astype(BF16)
    sums_ref[...] = norm_scale * lax.dot_general(
        jnp.concatenate(all_hops, axis=0),
        jnp.concatenate(all_up, axis=0),
        TN,
        preferred_element_type=F32,
    )


def backward_kernel(
    first_ref,
    far_g_ref,
    near_ref,
    own_ref,
    m_ref,
    proj_hbm,
    mix_hbm,
    weight_ref,
    swapped_ref,
    hops_ref,
    props_ref,
    adjt_ref,
    score_ref,
    rdeg_ref,
    sums_ref,
    g_ref,
    q_ref,
    back_ref,
    off_ref,
    offrow_ref,
    dm_ref,
    mix_ref,
    proj_ref,
    sems,
):
    copies = (
        pltpu.make_async_copy(mix_hbm, mix_ref, sems.at[0]),
        pltpu.make_async_copy(proj_hbm, proj_ref, sems.at[1]),
    )
    for copy in copies:
        copy.start()
    b = BLOCK
    nodes, width = m_ref.shape
    rim = far_g_ref.shape[0]
    own_units = nodes // b
    units = own_units + 2 * HALO
    reach = HALO + 1
    row = 2 * width
    keep = 1.0 - KEEP_INPUT
    far_place, near_place = rim_places(rim, nodes)
    g_ref[far_place, :] = far_g_ref[...]
    g_ref[near_place, :] = near_ref[:, 3 * width :]
    g_ref[rim : rim + nodes, :] = own_ref[:, 3 * width :]
    firsts = [first_ref[u] for u in range(units)]
    windows = [pl.ds(pl.multiple_of(firsts[u] * b, b), reach * b) for u in range(units)]
    for copy in copies:
        copy.wait()
    mixed = jnp.concatenate([mix_ref[2], mix_ref[1]], axis=0)
    for r in range(0, units, 2):
        rows = unit_rows(r, 2)
        for s in range(2):
            cut = slice(s * width, (s + 1) * width)
            back = lax.dot_general(g_ref[rows, cut], mixed, NT, preferred_element_type=F32)
            q_ref[rows, row + s * width : row + (s + 1) * width] = (
                keep * back[:, :width] * rdeg_ref[rows, :]
            ).astype(BF16)
            back_ref[rows, cut] = back[:, width:]
    for u in range(units):
        rows = unit_rows(u)
        carried = jnp.dot(
            adjt_ref[rows, :], q_ref[windows[u], row:], preferred_element_type=F32
        )
        grad_one = (keep * (back_ref[rows, :] + carried) * twice(rdeg_ref[rows, :])).astype(BF16)
        q_ref[rows, :row] = grad_one
        inner = grad_one.astype(F32) * props_ref[rows, :row].astype(F32) + q_ref[
            rows, row:
        ].astype(F32) * props_ref[rows, row:].astype(F32)
        offset = jnp.broadcast_to(jnp.sum(inner, axis=1, keepdims=True), (b, width))
        off_ref[rows, :] = offset
        offrow_ref[u] = jnp.transpose(offset)[:8]

    own_first = HALO
    for u in range(own_first, own_first + own_units):
        rows = unit_rows(u)
        local = unit_rows(u - own_first)
        grad_m = jnp.zeros((b, width), F32)
        for k in range(0, reach, 2):
            columns = pl.ds(pl.multiple_of((firsts[u] + k) * b, b), 2 * b)
            inner = lax.dot_general(
                q_ref[rows, :], hops_ref[columns, :], NT, preferred_element_type=F32
            )
            inner_t = lax.dot_general(
                hops_ref[rows, :], q_ref[columns, :], NT, preferred_element_type=F32
            )
            squashed = score_ref[local, unit_rows(k, 2)]
            offset_t = jnp.concatenate(
                [offrow_ref[firsts[u] + k + i, 0:1, :] for i in range(2)], axis=1
            )
            chosen = jnp.where(
                squashed > 0.0, inner - twice(off_ref[rows, :]), inner_t - offset_t
            )
            pair = (6.0 * squashed * (1.0 - squashed * squashed) * chosen).astype(BF16)
            grad_m = grad_m + jnp.dot(
                pair, swapped_ref[columns, :], preferred_element_type=F32
            )
        mine = m_ref[local, :]
        dm_ref[local, :] = 3.0 * (1.0 - mine * mine) * grad_m
    grad = lax.dot_general(
        dm_ref[...],
        block_diagonal(proj_ref[...]),
        NT,
        precision=HIGHEST,
        preferred_element_type=F32,
    ).astype(BF16)
    groups = sums_ref.shape[0]
    rows_v = nodes // groups
    rows_w = weight_ref.shape[0] // groups
    for k in range(groups):
        sums_ref[k, :rows_v, :] = grad[k * rows_v : (k + 1) * rows_v]
        sums_ref[k, rows_v:, :] = weight_ref[k * rows_w : (k + 1) * rows_w].astype(BF16)


def finish_kernel(got_ref, vector_ref, weight_ref):
    groups = got_ref.shape[0]
    rows_v = vector_ref.shape[0] // groups
    rows_w = weight_ref.shape[0] // groups
    for k in range(groups):
        got = got_ref[k].astype(F32)
        vector_ref[k * rows_v : (k + 1) * rows_v, :] = got[:rows_v]
        weight_ref[k * rows_w : (k + 1) * rows_w, :] = got[rows_v:]


def device_groups(counts, kept):
    strides = [math.prod(counts[i + 1 :]) for i in range(len(counts))]

    def spread(axes):
        numbers = [0]
        for i in axes:
            numbers = [n + k * strides[i] for n in numbers for k in range(counts[i])]
        return numbers

    others = [i for i in range(len(counts)) if i not in kept]
    return [[base + k for k in spread(kept)] for base in spread(others)]


def body(features, node_vectors, projections, mix_weight, region_sizes, cotangent):
    nodes, _, steps, width = features.shape
    axes = ("node", "win")
    node_count, win_count = lax.axis_size("node"), lax.axis_size("win")
    own_units = nodes // BLOCK
    units = own_units + 2 * HALO
    rim = HALO * BLOCK
    flat = nodes * steps
    row = steps * width
    in_vmem = pl.BlockSpec(memory_space=pltpu.VMEM)
    in_hbm = pl.BlockSpec(memory_space=pltpu.HBM)
    features, cotangent = features.reshape(flat, width), cotangent.reshape(flat, width)
    features, cotangent, node_vectors, projections, mix_weight = (
        pltpu.with_memory_space_constraint(array, pltpu.HBM)
        for array in (features, cotangent, node_vectors, projections, mix_weight)
    )
    own, far, far_g, near, learned = pl.pallas_call(
        pack_kernel,
        name="pack",
        in_specs=[in_hbm] * 4,
        out_shape=(
            jax.ShapeDtypeStruct((nodes, 5 * width), BF16),
            jax.ShapeDtypeStruct((rim, 3 * width), BF16),
            jax.ShapeDtypeStruct((rim, 2 * width), BF16),
            jax.ShapeDtypeStruct((rim, 5 * width), BF16),
            jax.ShapeDtypeStruct((nodes, width), F32),
        ),
        scratch_shapes=[
            pltpu.VMEM((flat, width), BF16),
            pltpu.VMEM((flat, width), BF16),
            pltpu.VMEM((nodes, width), F32),
            pltpu.VMEM(projections.shape, F32),
            pltpu.VMEM((flat, width), F32),
            pltpu.SemaphoreType.DMA((4,)),
        ],
        compiler_params=pltpu.CompilerParams(vmem_limit_bytes=16 << 20),
    )(features, cotangent, node_vectors, projections)
    border = [(i, i + 1) for i in range(1, node_count - 1, 2)]
    inside = [(i, i + 1) for i in range(0, node_count, 2)]
    across = border + [(j, i) for i, j in border]
    far = lax.ppermute(far, "node", across)
    near = lax.ppermute(near, "node", inside + [(j, i) for i, j in inside])
    far_g = lax.ppermute(far_g, "node", across)
    lead = lax.axis_index("node") * own_units - HALO
    place = jnp.arange(units, dtype=jnp.int32)
    unit = lead + place
    ends = jnp.cumsum(region_sizes)
    passed = (ends[None, :] <= unit[:, None]).astype(jnp.int32)
    in_range = (unit >= 0) & (unit < node_count * own_units)
    region = jnp.where(in_range, jnp.sum(passed, axis=1), -1)
    first = jnp.sum(passed * region_sizes[None, :], axis=1) - lead
    first = jnp.clip(
        first, jnp.maximum(place - HALO, 0), jnp.minimum(place, units - HALO - 1)
    )

    span = units * BLOCK
    y_far, y_near = 2, 2
    inner_count = node_count // (y_far * y_near)
    groups = y_far * win_count
    rows_v = nodes // groups
    rows_w = 3 * width // groups
    reach = (HALO + 1) * BLOCK
    in_smem = pl.BlockSpec(memory_space=pltpu.SMEM)
    out, weights, *kept = pl.pallas_call(
        partial(forward_kernel, 1.0 / math.sqrt(flat * node_count * win_count)),
        name="forward",
        in_specs=[in_smem] * 2 + [in_vmem] * 3 + [in_hbm],
        out_shape=(
            jax.ShapeDtypeStruct((flat, width), BF16),
            jax.ShapeDtypeStruct((3 * width, width), F32),
            jax.ShapeDtypeStruct((span, width), BF16),
            jax.ShapeDtypeStruct((span, 2 * row), BF16),
            jax.ShapeDtypeStruct((span, 2 * row), BF16),
            jax.ShapeDtypeStruct((span, reach), BF16),
            jax.ShapeDtypeStruct((nodes, reach), F32),
            jax.ShapeDtypeStruct((span, width), F32),
        ),
        scratch_shapes=[
            pltpu.VMEM((span, width), BF16),
            pltpu.VMEM((span, reach), BF16),
            pltpu.VMEM((nodes, row), BF16),
            pltpu.VMEM((flat, width), F32),
            pltpu.VMEM(mix_weight.shape, BF16),
            pltpu.SemaphoreType.DMA,
        ],
        compiler_params=pltpu.CompilerParams(vmem_limit_bytes=24 << 20),
        cost_estimate=pl.CostEstimate(
            flops=6 * span * reach * row, bytes_accessed=8 << 20, transcendentals=span * reach
        ),
    )(region, first, far, near, own, mix_weight)
    sums = pl.pallas_call(
        backward_kernel,
        name="backward",
        in_specs=[in_smem] + [in_vmem] * 4 + [in_hbm] * 2 + [in_vmem] * 7,
        out_shape=jax.ShapeDtypeStruct((groups, rows_v + rows_w, width), BF16),
        scratch_shapes=[
            pltpu.VMEM((span, row), BF16),
            pltpu.VMEM((span, 2 * row), BF16),
            pltpu.VMEM((span, row), F32),
            pltpu.VMEM((span, width), F32),
            pltpu.VMEM((units, 8, width), F32),
            pltpu.VMEM((nodes, width), F32),
            pltpu.VMEM(mix_weight.shape, BF16),
            pltpu.VMEM(projections.shape, F32),
            pltpu.SemaphoreType.DMA((2,)),
        ],
        compiler_params=pltpu.CompilerParams(vmem_limit_bytes=24 << 20),
        cost_estimate=pl.CostEstimate(
            flops=6 * span * reach * row, bytes_accessed=8 << 20, transcendentals=0
        ),
    )(first, far_g, near, own, learned, projections, mix_weight, weights, *kept)

    counts = (y_far, y_near, inner_count, win_count)
    outer_groups = device_groups(counts, (0, 3))
    inner_groups = device_groups(counts, (1, 2))
    exchange = partial(
        lax.all_to_all, axis_name=axes, split_axis=0, concat_axis=0, tiled=True
    )
    got = exchange(sums, axis_index_groups=outer_groups).astype(F32)
    vector_sum = jnp.sum(
        got[:, :rows_v].reshape(y_far, win_count, rows_v, width), axis=1
    ).astype(BF16)
    weight_sum = jnp.sum(got[:, rows_v:], axis=0).astype(BF16)
    shares = jnp.broadcast_to(weight_sum[None], (y_near * inner_count, rows_w, width))
    vector_sum, shares = lax.optimization_barrier((vector_sum, shares))
    got = exchange(shares, axis_index_groups=inner_groups).astype(F32)
    weight_sum = jnp.sum(got, axis=0).astype(BF16)
    back = jnp.concatenate(
        [
            jnp.broadcast_to(
                vector_sum[:, None], (y_far, win_count, rows_v, width)
            ).reshape(groups, rows_v, width),
            jnp.broadcast_to(weight_sum[None], (groups, rows_w, width)),
        ],
        axis=1,
    )
    got = exchange(back, axis_index_groups=outer_groups)
    vector_grad, weight_grad = pl.pallas_call(
        finish_kernel,
        name="finish",
        in_specs=[in_vmem],
        out_shape=(
            jax.ShapeDtypeStruct((nodes, width), F32),
            jax.ShapeDtypeStruct((3 * width, width), F32),
        ),
        compiler_params=pltpu.CompilerParams(vmem_limit_bytes=8 << 20),
    )(got)
    weight_grad = weight_grad.reshape(3, width, width)
    return (out.reshape(nodes, 1, steps, width), vector_grad, weight_grad)


def solution(mesh):
    placed = (
        P("node", "win", None, None),
        P("node", None),
        P(),
        P(),
        P(),
        P("node", "win", None, None),
    )
    return jax.shard_map(
        body,
        mesh=mesh,
        in_specs=placed,
        out_specs=(P("node", "win", None, None), P("node", None), P()),
        check_vma=False,
    )
```

time: 80.8 us -> 87.8 us (1.087)
  Pallas kernels: 10.5 us -> 16.4 us
    pallas_call x1 -> x2, Pallas kernels: 8.09 us -> 14 us  [the longest x1 7.22 us: body(): pl.pallas_call(partial(forward_kernel, 1.0 / math.sqrt(flat * node_count...]
    ppermute x1 -> x2, starting transfers between devices: 5.37 us -> 7.29 us  [the longest x1 5.37 us: body(): far_g = lax.ppermute(far_g, 'node', across)]
    ppermute x1, starting transfers between devices: 4.06 us -> 2.8 us  [body(): near = lax.ppermute(near, 'node', inside + [(j, i) for i, j in inside])]
    all_to_all x1, blocking collectives: 19.7 us -> 18.8 us  [body(): got = exchange(shares, axis_index_groups=inner_groups).astype(F32)]
  transfers between devices with their start and end apart: 2 -> 3, of which waited for: 1 -> 1; matrix products, arithmetic and copies ran while one was open for 1% -> 2% of each run, Pallas kernels for 0% -> 8%
where the time goes in v4:
time: 87.8 us; the launch traced here: 87.4 us
  blocking collectives  56.6 us (64%)
  Pallas kernels  16.4 us (19%)
  starting transfers between devices  10.1 us (12%)
  waiting for transfers between devices  1.38 us (2%)
  other arithmetic  1.27 us (1%)
    all_to_all x1, blocking collectives, body(): got = exchange(sums, axis_index_groups=outer_groups).astype(F32)  23.4 us
    all_to_all x1, blocking collectives, body(): got = exchange(shares, axis_index_groups=inner_groups).astype(F32)  18.8 us
    all_to_all x1, blocking collectives, body(): got = exchange(back, axis_index_groups=outer_groups)  14.4 us
    pallas_call x1, Pallas kernels, body(): pl.pallas_call(partial(forward_kernel, 1.0 / math.sqrt(flat * node_count...  7.22 us
    pallas_call x1, Pallas kernels, body(): pl.pallas_call(backward_kernel, name='backward', in_specs=[in_smem] + [in...  6.81 us
    ppermute x1, starting transfers between devices, body(): far_g = lax.ppermute(far_g, 'node', across)  5.37 us
    ppermute x1, starting transfers between devices, body(): near = lax.ppermute(near, 'node', inside + [(j, i) for i, j in inside])  2.8 us
    ppermute x1, starting transfers between devices, body(): far = lax.ppermute(far, 'node', across)  1.92 us
  transfers between devices with their start and end apart: 3, of which 1 were waited for; matrix products, arithmetic and copies ran while one was open for 2% of the time, Pallas kernels for 8%

profile of v4, /device:TPU:1, one launch (start us, length us, event | category | flops | bytes accessed | tf_op | source)
XLA Modules:
  0.0 87.4 jit_solution(11948732859975436682)
XLA Ops:
  0.6 1.6 %pack.1 = (bf16[512,640]{1,0:T(8,128)(2,1)S(1)}, bf16[384,384]{1,0:T(8,128)(2,1)S(1)}, bf16[384,256]{1,0:T(8,128)(2,1)S(1)}, bf16[384,640]{1,0:T(8,128)(2,1)S(1)}, f32[512,128]{1,0:T(8,128)S(1)}) custom-call(bf16[1024,128]{1,0:T(8,128)(2,1)} %bitcast.11, bf16[1024,128]{1,0:T(8,128)(2,1)} %bitcast.12, f32[512,128]{1,0:T(8,128)} %nv_hbm.1, f32[2,64,64]{2,1,0:T(8,128)} %proj_hbm.3), custom_call_target="tpu_custom_call" | custom-call | tf_op jit(solution)/shard_map/pack/pallas_call | solution.py:369
  2.3 5.4 %collective-permute-start.2 = (bf16[384,256]{1,0:T(8,128)(2,1)S(1)}, bf16[384,256]{1,0:T(8,128)(2,1)S(1)}, u32[]{:S(2)}, u32[]{:S(2)}) collective-permute-start(bf16[384,256]{1,0:T(8,128)(2,1)S(1)} %get-tuple-element.24), channel_id=1, source_target_pairs={{8,16},{24,32},{40,48},{56,64},{72,80},{88,96},{104,112},{120,128}... | collective-permute-start | bytes 589832 | tf_op jit(solution)/shard_map/ppermute | solution.py:395
  7.6 1.9 %collective-permute-start = (bf16[384,384]{1,0:T(8,128)(2,1)S(1)}, bf16[384,384]{1,0:T(8,128)(2,1)S(1)}, u32[]{:S(2)}, u32[]{:S(2)}) collective-permute-start(bf16[384,384]{1,0:T(8,128)(2,1)S(1)} %get-tuple-element.20), channel_id=1, source_target_pairs={{8,16},{24,32},{40,48},{56,64},{72,80},{88,96},{104,112},{120,128}... | collective-permute-start | bytes 884744 | tf_op jit(solution)/shard_map/ppermute | solution.py:393
  9.6 2.8 %collective-permute-start.1 = (bf16[384,640]{1,0:T(8,128)(2,1)S(1)}, bf16[384,640]{1,0:T(8,128)(2,1)S(1)}, u32[]{:S(2)}, u32[]{:S(2)}) collective-permute-start(bf16[384,640]{1,0:T(8,128)(2,1)S(1)} %get-tuple-element.21), channel_id=1, source_target_pairs={{0,8},{16,24},{32,40},{48,56},{64,72},{80,88},{96,104},{112,120},{... | collective-permute-start | bytes 1474568 | tf_op jit(solution)/shard_map/ppermute | solution.py:394
  12.4 0.8 copy.13
  13.2 0.2 reduce-window.8
  13.3 0.1 reduce.1
  13.4 0.8 fusion.1
  14.3 1.4 %collective-permute-done.far_ref = bf16[384,384]{1,0:T(8,128)(2,1)S(1)} collective-permute-done((bf16[384,384]{1,0:T(8,128)(2,1)S(1)}, bf16[384,384]{1,0:T(8,128)(2,1)S(1)}, u32[]{:S(2)}, u32[]{:S(2)}) %collective-permute-start) | collective-permute-done | bytes 294944 | tf_op jit(solution)/shard_map/ppermute | solution.py:393
  15.7 0.0 collective-permute-done.1.near_ref
  15.7 7.2 %forward.1 = (bf16[1024,128]{1,0:T(8,128)(2,1)}, f32[384,128]{1,0:T(8,128)S(1)}, bf16[1280,128]{1,0:T(8,128)(2,1)S(1)}, bf16[1280,512]{1,0:T(8,128)(2,1)S(1)}, b...) custom-call(s32[10]{0:T(128)S(1)} %and_select_fusion.region_ref, ...), custom_call_target="tpu_custom_call" | custom-call | flops 1006632960 | bytes 8388608 | tf_op jit(solution)/shard_map/forward/pallas_call | solution.py:416
  22.9 0.0 collective-permute-done.2.far_g_ref
  22.9 6.8 %backward.1 = bf16[16,56,128]{2,1,0:T(8,128)(2,1)S(1)} custom-call(s32[10]{0:T(128)S(1)} %maximum_minimum_fusion.first_ref, bf16[384,256]{1,0:T(8,128)(2,1)S(1)} %collective-permute-done.2.far_g_ref, bf16[384,640]{1,0:T(8,128)(2,1)S(1)} %collective-permute-done.1.near_ref, bf16[512,640]{1,0:T(8,128)(2,1)S(1)} %get-tuple-element.22.own_ref, ...), custom_call_target="tpu_custom_call" | custom-call | flops 1006632960 | bytes 8388608 | tf_op jit(solution)/shard_map/backward/pallas_call | solution.py:443
  29.7 23.4 %all_to_all.15 = bf16[16,56,128]{2,1,0:T(8,128)(2,1)S(1)} all-to-all(bf16[16,56,128]{2,1,0:T(8,128)(2,1)S(1)} %backward.1), channel_id=1, replica_groups={{0,1,2,3,4,5,6,7,256,257,258,259,260,261,262,263},{8,9,10,11,12,13,14,1..., dimensions={0} | all-to-all | bytes 458752 | tf_op jit(solution)/shard_map/all_to_all | solution.py:471
  53.2 18.8 %all_to_all.16 = bf16[32,24,128]{2,1,0:T(8,128)(2,1)S(1)} all-to-all(bf16[32,24,128]{2,1,0:T(8,128)(2,1)S(1)} %broadcast_in_dim.11), channel_id=1, replica_groups={{0,8,16,24,32,40,48,56,64,72,80,88,96,104,112,120,128,136,144,152,160,1..., dimensions={0} | all-to-all | bytes 393216 | tf_op jit(solution)/shard_map/all_to_all | solution.py:478
  72.1 14.4 %all_to_all.17.got_ref = bf16[16,56,128]{2,1,0:T(8,128)(2,1)S(1)} all-to-all(bf16[16,56,128]{2,1,0:T(8,128)(2,1)S(1)} %pad_maximum_fusion), channel_id=1, replica_groups={{0,1,2,3,4,5,6,7,256,257,258,259,260,261,262,263},{8,9,10,11,12,13,14,1..., dimensions={0} | all-to-all | bytes 458752 | tf_op jit(solution)/shard_map/all_to_all | solution.py:489
  86.6 0.8 finish.1
  (11 shorter events, 0.2 us)
Async XLA Ops:
  2.3 20.7 %collective-permute-start.2 = (bf16[384,256]{1,0:T(8,128)(2,1)S(1)}, bf16[384,256]{1,0:T(8,128)(2,1)S(1)}, u32[]{:S(2)}, u32[]{:S(2)}) collective-permute-start(bf16[384,256]{1,0:T(8,128)(2,1)S(1)} %get-tuple-element.24), channel_id=1, source_target_pairs={{8,16},{24,32},{40,48},{56,64},{72,80},{88,96},{104,112},{120,128}... | collective-permute-start | bytes 589832 | tf_op jit(solution)/shard_map/ppermute | solution.py:395
  7.6 8.0 %collective-permute-start = (bf16[384,384]{1,0:T(8,128)(2,1)S(1)}, bf16[384,384]{1,0:T(8,128)(2,1)S(1)}, u32[]{:S(2)}, u32[]{:S(2)}) collective-permute-start(bf16[384,384]{1,0:T(8,128)(2,1)S(1)} %get-tuple-element.20), channel_id=1, source_target_pairs={{8,16},{24,32},{40,48},{56,64},{72,80},{88,96},{104,112},{120,128}... | collective-permute-start | bytes 884744 | tf_op jit(solution)/shard_map/ppermute | solution.py:393
  9.6 6.1 %collective-permute-start.1 = (bf16[384,640]{1,0:T(8,128)(2,1)S(1)}, bf16[384,640]{1,0:T(8,128)(2,1)S(1)}, u32[]{:S(2)}, u32[]{:S(2)}) collective-permute-start(bf16[384,640]{1,0:T(8,128)(2,1)S(1)} %get-tuple-element.21), channel_id=1, source_target_pairs={{0,8},{16,24},{32,40},{48,56},{64,72},{80,88},{96,104},{112,120},{... | collective-permute-start | bytes 1474568 | tf_op jit(solution)/shard_map/ppermute | solution.py:394

commit v5 on v4

--- a/solution.py
+++ b/solution.py
@@ -85,8 +85,21 @@
     )
 
 
+def beside(left, right):
+    return jnp.concatenate([left, right], axis=1)
+
+
 def twice(values):
-    return jnp.concatenate([values, values], axis=1)
+    return beside(values, values)
+
+
+def turned(learned):
+    width = learned.shape[1]
+    half = width // 2
+    i = lax.broadcasted_iota(jnp.int32, (width, width), 0)
+    j = lax.broadcasted_iota(jnp.int32, (width, width), 1)
+    turn = jnp.where(i == j + half, 1.0, 0.0) - jnp.where(j == i + half, 1.0, 0.0)
+    return jnp.dot(learned, turn.astype(BF16), preferred_element_type=F32).astype(BF16)
 
 
 def forward_kernel(
@@ -100,8 +113,10 @@
     out_ref,
     sums_ref,
     swapped_ref,
-    hops_ref,
-    props_ref,
+    x_ref,
+    one_ref,
+    prop_one_ref,
+    prop_two_ref,
     adjt_ref,
     score_ref,
     rdeg_ref,
@@ -120,17 +135,13 @@
     own_units = nodes // b
     units = own_units + 2 * HALO
     reach = HALO + 1
-    row = 2 * width
-    half = width // 2
     far_place, near_place = rim_places(rim, nodes)
     own_place = pl.ds(rim, nodes)
     for place, source in ((far_place, far_ref), (own_place, own_ref), (near_place, near_ref)):
         learned = source[:, :width]
         learned_ref[place, :] = learned
-        swapped_ref[place, :] = jnp.concatenate(
-            [learned[:, half:], -learned[:, :half]], axis=1
-        )
-        hops_ref[place, :row] = source[:, width : 3 * width]
+        swapped_ref[place, :] = turned(learned)
+        x_ref[place, :] = source[:, width : 3 * width]
 
     firsts = [first_ref[u] for u in range(units)]
     eye = (
@@ -150,8 +161,8 @@
                 NT,
                 preferred_element_type=F32,
             )
-            same = jnp.where((region_ref[other] == mine) & (mine >= 0), 1.0, 0.0)
-            squashed = jnp.tanh(3.0 * scores) * same
+            same = jnp.where((region_ref[other] == mine) & (mine >= 0), 3.0, 0.0)
+            squashed = jnp.tanh(scores * same)
             positive = jnp.maximum(squashed, 0.0)
             negative = jnp.minimum(squashed, 0.0)
             forward = positive * positive
@@ -161,30 +172,33 @@
             adj_ref[rows, columns] = forward.astype(BF16)
             adjt_ref[rows, columns] = (negative * negative).astype(BF16)
             total = total + forward
+        degree = 1.0 + jnp.sum(total, axis=1, keepdims=True)
+        rdeg_ref[rows, :] = jnp.broadcast_to(1.0 / degree, (b, width))
+    for u in range(units):
+        rows = unit_rows(u)
         diagonal = pl.ds(pl.multiple_of((u - firsts[u]) * b, b), b)
         adj_ref[rows, diagonal] = (adj_ref[rows, diagonal].astype(F32) + eye).astype(BF16)
         adjt_ref[rows, diagonal] = (adjt_ref[rows, diagonal].astype(F32) + eye).astype(BF16)
-        degree = 1.0 + jnp.sum(total, axis=1, keepdims=True)
-        rdeg_ref[rows, :] = jnp.broadcast_to(1.0 / degree, (b, width))
 
     keep = 1.0 - KEEP_INPUT
     windows = [pl.ds(pl.multiple_of(firsts[u] * b, b), reach * b) for u in range(units)]
-    for hop in range(2):
-        source = slice(hop * row, (hop + 1) * row)
-        for u in range(units):
-            rows = unit_rows(u)
-            prop = jnp.dot(
-                adj_ref[rows, :], hops_ref[windows[u], source], preferred_element_type=F32
-            ) * twice(rdeg_ref[rows, :])
-            props_ref[rows, source] = prop.astype(BF16)
-            if hop == 0:
-                hops_ref[rows, row:] = (
-                    KEEP_INPUT * hops_ref[rows, :row].astype(F32) + keep * prop
-                ).astype(BF16)
-            elif own_first <= u < own_last:
-                two_ref[unit_rows(u - own_first), :] = (
-                    KEEP_INPUT * hops_ref[rows, :row].astype(F32) + keep * prop
-                ).astype(BF16)
+    for u in range(units):
+        rows = unit_rows(u)
+        prop = jnp.dot(
+            adj_ref[rows, :], x_ref[windows[u], :], preferred_element_type=F32
+        ) * twice(rdeg_ref[rows, :])
+        prop_one_ref[rows, :] = prop.astype(BF16)
+        one_ref[rows, :] = (KEEP_INPUT * x_ref[rows, :].astype(F32) + keep * prop).astype(BF16)
+    for u in range(units):
+        rows = unit_rows(u)
+        prop = jnp.dot(
+            adj_ref[rows, :], one_ref[windows[u], :], preferred_element_type=F32
+        ) * twice(rdeg_ref[rows, :])
+        prop_two_ref[rows, :] = prop.astype(BF16)
+        if own_first <= u < own_last:
+            two_ref[unit_rows(u - own_first), :] = (
+                KEEP_INPUT * x_ref[rows, :].astype(F32) + keep * prop
+            ).astype(BF16)
 
     mix_copy.wait()
     weights = jnp.concatenate([mix_ref[0], mix_ref[1], mix_ref[2]], axis=0)
@@ -193,12 +207,7 @@
         cut = slice(s * width, (s + 1) * width)
         all_hops.append(
             jnp.concatenate(
-                [
-                    hops_ref[own_place, cut],
-                    hops_ref[own_place, row + s * width : row + (s + 1) * width],
-                    two_ref[:, cut],
-                ],
-                axis=1,
+                [x_ref[own_place, cut], one_ref[own_place, cut], two_ref[:, cut]], axis=1
             )
         )
         all_up.append(own_ref[:, 3 * width + s * width : 3 * width + (s + 1) * width])
@@ -224,14 +233,17 @@
     mix_hbm,
     weight_ref,
     swapped_ref,
-    hops_ref,
-    props_ref,
+    x_ref,
+    one_ref,
+    prop_one_ref,
+    prop_two_ref,
     adjt_ref,
     score_ref,
     rdeg_ref,
     sums_ref,
     g_ref,
-    q_ref,
+    q_one_ref,
+    q_two_ref,
     back_ref,
     off_ref,
     offrow_ref,
@@ -252,7 +264,6 @@
     own_units = nodes // b
     units = own_units + 2 * HALO
     reach = HALO + 1
-    row = 2 * width
     keep = 1.0 - KEEP_INPUT
     far_place, near_place = rim_places(rim, nodes)
     g_ref[far_place, :] = far_g_ref[...]
@@ -268,20 +279,20 @@
         for s in range(2):
             cut = slice(s * width, (s + 1) * width)
             back = lax.dot_general(g_ref[rows, cut], mixed, NT, preferred_element_type=F32)
-            q_ref[rows, row + s * width : row + (s + 1) * width] = (
+            q_two_ref[rows, cut] = (
                 keep * back[:, :width] * rdeg_ref[rows, :]
             ).astype(BF16)
             back_ref[rows, cut] = back[:, width:]
     for u in range(units):
         rows = unit_rows(u)
         carried = jnp.dot(
-            adjt_ref[rows, :], q_ref[windows[u], row:], preferred_element_type=F32
+            adjt_ref[rows, :], q_two_ref[windows[u], :], preferred_element_type=F32
         )
         grad_one = (keep * (back_ref[rows, :] + carried) * twice(rdeg_ref[rows, :])).astype(BF16)
-        q_ref[rows, :row] = grad_one
-        inner = grad_one.astype(F32) * props_ref[rows, :row].astype(F32) + q_ref[
-            rows, row:
-        ].astype(F32) * props_ref[rows, row:].astype(F32)
+        q_one_ref[rows, :] = grad_one
+        inner = grad_one.astype(F32) * prop_one_ref[rows, :].astype(F32) + q_two_ref[
+            rows, :
+        ].astype(F32) * prop_two_ref[rows, :].astype(F32)
         offset = jnp.broadcast_to(jnp.sum(inner, axis=1, keepdims=True), (b, width))
         off_ref[rows, :] = offset
         offrow_ref[u] = jnp.transpose(offset)[:8]
@@ -294,10 +305,16 @@
         for k in range(0, reach, 2):
             columns = pl.ds(pl.multiple_of((firsts[u] + k) * b, b), 2 * b)
             inner = lax.dot_general(
-                q_ref[rows, :], hops_ref[columns, :], NT, preferred_element_type=F32
+                beside(q_one_ref[rows, :], q_two_ref[rows, :]),
+                beside(x_ref[columns, :], one_ref[columns, :]),
+                NT,
+                preferred_element_type=F32,
             )
             inner_t = lax.dot_general(
-                hops_ref[rows, :], q_ref[columns, :], NT, preferred_element_type=F32
+                beside(x_ref[rows, :], one_ref[rows, :]),
+                beside(q_one_ref[columns, :], q_two_ref[columns, :]),
+                NT,
+                preferred_element_type=F32,
             )
             squashed = score_ref[local, unit_rows(k, 2)]
             offset_t = jnp.concatenate(
@@ -401,9 +418,7 @@
     in_range = (unit >= 0) & (unit < node_count * own_units)
     region = jnp.where(in_range, jnp.sum(passed, axis=1), -1)
     first = jnp.sum(passed * region_sizes[None, :], axis=1) - lead
-    first = jnp.clip(
-        first, jnp.maximum(place - HALO, 0), jnp.minimum(place, units - HALO - 1)
-    )
+    first = jnp.clip(first, jnp.maximum(place - HALO, 0), jnp.minimum(place, units - HALO - 1))
 
     span = units * BLOCK
     y_far, y_near = 2, 2
@@ -421,8 +436,10 @@
             jax.ShapeDtypeStruct((flat, width), BF16),
             jax.ShapeDtypeStruct((3 * width, width), F32),
             jax.ShapeDtypeStruct((span, width), BF16),
-            jax.ShapeDtypeStruct((span, 2 * row), BF16),
-            jax.ShapeDtypeStruct((span, 2 * row), BF16),
+            jax.ShapeDtypeStruct((span, row), BF16),
+            jax.ShapeDtypeStruct((span, row), BF16),
+            jax.ShapeDtypeStruct((span, row), BF16),
+            jax.ShapeDtypeStruct((span, row), BF16),
             jax.ShapeDtypeStruct((span, reach), BF16),
             jax.ShapeDtypeStruct((nodes, reach), F32),
             jax.ShapeDtypeStruct((span, width), F32),
@@ -443,11 +460,12 @@
     sums = pl.pallas_call(
         backward_kernel,
         name="backward",
-        in_specs=[in_smem] + [in_vmem] * 4 + [in_hbm] * 2 + [in_vmem] * 7,
+        in_specs=[in_smem] + [in_vmem] * 4 + [in_hbm] * 2 + [in_vmem] * 9,
         out_shape=jax.ShapeDtypeStruct((groups, rows_v + rows_w, width), BF16),
         scratch_shapes=[
             pltpu.VMEM((span, row), BF16),
-            pltpu.VMEM((span, 2 * row), BF16),
+            pltpu.VMEM((span, row), BF16),
+            pltpu.VMEM((span, row), BF16),
             pltpu.VMEM((span, row), F32),
             pltpu.VMEM((span, width), F32),
             pltpu.VMEM((units, 8, width), F32),

time: 87.8 us -> 84.2 us (0.959)
  Pallas kernels: 16.4 us -> 12.9 us
    pallas_call x1, Pallas kernels: 7.22 us -> 5.17 us  [body(): pl.pallas_call(partial(forward_kernel, 1.0 / math.sqrt(flat * node_count...]
    pallas_call x1, Pallas kernels: 6.81 us -> 5.3 us  [body(): pl.pallas_call(backward_kernel, name='backward', in_specs=[in_smem] + [in...]
  transfers between devices with their start and end apart: 3 -> 3, of which waited for: 1 -> 1; matrix products, arithmetic and copies ran while one was open for 2% -> 2% of each run, Pallas kernels for 8% -> 6%
where the time goes in v5:
time: 84.2 us; the launch traced here: 83.8 us
  blocking collectives  56.6 us (67%)
  Pallas kernels  12.9 us (15%)
  starting transfers between devices  10.1 us (12%)
  waiting for transfers between devices  1.38 us (2%)
  other arithmetic  1.27 us (2%)
    all_to_all x1, blocking collectives, body(): got = exchange(sums, axis_index_groups=outer_groups).astype(F32)  23.4 us
    all_to_all x1, blocking collectives, body(): got = exchange(shares, axis_index_groups=inner_groups).astype(F32)  18.8 us
    all_to_all x1, blocking collectives, body(): got = exchange(back, axis_index_groups=outer_groups)  14.4 us
    ppermute x1, starting transfers between devices, body(): far_g = lax.ppermute(far_g, 'node', across)  5.37 us
    pallas_call x1, Pallas kernels, body(): pl.pallas_call(backward_kernel, name='backward', in_specs=[in_smem] + [in...  5.3 us
    pallas_call x1, Pallas kernels, body(): pl.pallas_call(partial(forward_kernel, 1.0 / math.sqrt(flat * node_count...  5.17 us
    ppermute x1, starting transfers between devices, body(): near = lax.ppermute(near, 'node', inside + [(j, i) for i, j in inside])  2.8 us
    ppermute x1, starting transfers between devices, body(): far = lax.ppermute(far, 'node', across)  1.92 us
  transfers between devices with their start and end apart: 3, of which 1 were waited for; matrix products, arithmetic and copies ran while one was open for 2% of the time, Pallas kernels for 6%

profile of v5, /device:TPU:1, one launch (start us, length us, event | category | flops | bytes accessed | tf_op | source)
XLA Modules:
  0.0 83.8 jit_solution(14210146447564877368)
XLA Ops:
  0.6 1.6 %pack.1 = (bf16[512,640]{1,0:T(8,128)(2,1)S(1)}, bf16[384,384]{1,0:T(8,128)(2,1)S(1)}, bf16[384,256]{1,0:T(8,128)(2,1)S(1)}, bf16[384,640]{1,0:T(8,128)(2,1)S(1)}, f32[512,128]{1,0:T(8,128)S(1)}) custom-call(bf16[1024,128]{1,0:T(8,128)(2,1)} %bitcast.11, bf16[1024,128]{1,0:T(8,128)(2,1)} %bitcast.12, f32[512,128]{1,0:T(8,128)} %nv_hbm.1, f32[2,64,64]{2,1,0:T(8,128)} %proj_hbm.3), custom_call_target="tpu_custom_call" | custom-call | tf_op jit(solution)/shard_map/pack/pallas_call | solution.py:386
  2.3 5.4 %collective-permute-start.2 = (bf16[384,256]{1,0:T(8,128)(2,1)S(1)}, bf16[384,256]{1,0:T(8,128)(2,1)S(1)}, u32[]{:S(2)}, u32[]{:S(2)}) collective-permute-start(bf16[384,256]{1,0:T(8,128)(2,1)S(1)} %get-tuple-element.26), channel_id=1, source_target_pairs={{8,16},{24,32},{40,48},{56,64},{72,80},{88,96},{104,112},{120,128}... | collective-permute-start | bytes 589832 | tf_op jit(solution)/shard_map/ppermute | solution.py:412
  7.6 1.9 %collective-permute-start = (bf16[384,384]{1,0:T(8,128)(2,1)S(1)}, bf16[384,384]{1,0:T(8,128)(2,1)S(1)}, u32[]{:S(2)}, u32[]{:S(2)}) collective-permute-start(bf16[384,384]{1,0:T(8,128)(2,1)S(1)} %get-tuple-element.22), channel_id=1, source_target_pairs={{8,16},{24,32},{40,48},{56,64},{72,80},{88,96},{104,112},{120,128}... | collective-permute-start | bytes 884744 | tf_op jit(solution)/shard_map/ppermute | solution.py:410
  9.6 2.8 %collective-permute-start.1 = (bf16[384,640]{1,0:T(8,128)(2,1)S(1)}, bf16[384,640]{1,0:T(8,128)(2,1)S(1)}, u32[]{:S(2)}, u32[]{:S(2)}) collective-permute-start(bf16[384,640]{1,0:T(8,128)(2,1)S(1)} %get-tuple-element.23), channel_id=1, source_target_pairs={{0,8},{16,24},{32,40},{48,56},{64,72},{80,88},{96,104},{112,120},{... | collective-permute-start | bytes 1474568 | tf_op jit(solution)/shard_map/ppermute | solution.py:411
  12.4 0.8 copy.13
  13.2 0.2 reduce-window.8
  13.3 0.1 reduce.1
  13.4 0.8 %fusion.1 = (s32[10]{0:T(128)S(1)}, s32[10]{0:T(128)S(1)}) fusion(s32[128]{0:T(128)} %param.10, s32[128]{0:T(128)S(1)} %reduce.1, s32[10]{0:T(128)S(1)} %iota_add_fusion), kind=kLoop, calls=%fused_computation.6 | loop fusion | flops 6380 | bytes 1144 | tf_op jit(solution)/shard_map/reduce_sum | solution.py:420
  14.3 1.4 %collective-permute-done.far_ref = bf16[384,384]{1,0:T(8,128)(2,1)S(1)} collective-permute-done((bf16[384,384]{1,0:T(8,128)(2,1)S(1)}, bf16[384,384]{1,0:T(8,128)(2,1)S(1)}, u32[]{:S(2)}, u32[]{:S(2)}) %collective-permute-start) | collective-permute-done | bytes 294944 | tf_op jit(solution)/shard_map/ppermute | solution.py:410
  15.7 0.0 collective-permute-done.1.near_ref
  15.7 5.2 %forward.1 = (bf16[1024,128]{1,0:T(8,128)(2,1)}, f32[384,128]{1,0:T(8,128)S(1)}, bf16[1280,128]{1,0:T(8,128)(2,1)S(1)}, bf16[1280,256]{1,0:T(8,128)(2,1)S(1)}, b...) custom-call(s32[10]{0:T(128)S(1)} %and_select_fusion.region_ref, ...), custom_call_target="tpu_custom_call" | custom-call | flops 1006632960 | bytes 8388608 | tf_op jit(solution)/shard_map/forward/pallas_call | solution.py:431
  20.9 0.0 collective-permute-done.2.far_g_ref
  20.9 5.3 %backward.1 = bf16[16,56,128]{2,1,0:T(8,128)(2,1)S(1)} custom-call(s32[10]{0:T(128)S(1)} %maximum_minimum_fusion.first_ref, bf16[384,256]{1,0:T(8,128)(2,1)S(1)} %collective-permute-done.2.far_g_ref, bf16[384,640]{1,0:T(8,128)(2,1)S(1)} %collective-permute-done.1.near_ref, bf16[512,640]{1,0:T(8,128)(2,1)S(1)} %get-tuple-element.24.own_ref, ...), custom_call_target="tpu_custom_call" | custom-call | flops 1006632960 | bytes 8388608 | tf_op jit(solution)/shard_map/backward/pallas_call | solution.py:460
  26.2 23.4 %all_to_all.15 = bf16[16,56,128]{2,1,0:T(8,128)(2,1)S(1)} all-to-all(bf16[16,56,128]{2,1,0:T(8,128)(2,1)S(1)} %backward.1), channel_id=1, replica_groups={{0,1,2,3,4,5,6,7,256,257,258,259,260,261,262,263},{8,9,10,11,12,13,14,1..., dimensions={0} | all-to-all | bytes 458752 | tf_op jit(solution)/shard_map/all_to_all | solution.py:489
  49.7 18.8 %all_to_all.16 = bf16[32,24,128]{2,1,0:T(8,128)(2,1)S(1)} all-to-all(bf16[32,24,128]{2,1,0:T(8,128)(2,1)S(1)} %broadcast_in_dim.11), channel_id=1, replica_groups={{0,8,16,24,32,40,48,56,64,72,80,88,96,104,112,120,128,136,144,152,160,1..., dimensions={0} | all-to-all | bytes 393216 | tf_op jit(solution)/shard_map/all_to_all | solution.py:496
  68.6 14.4 %all_to_all.17.got_ref = bf16[16,56,128]{2,1,0:T(8,128)(2,1)S(1)} all-to-all(bf16[16,56,128]{2,1,0:T(8,128)(2,1)S(1)} %pad_maximum_fusion), channel_id=1, replica_groups={{0,1,2,3,4,5,6,7,256,257,258,259,260,261,262,263},{8,9,10,11,12,13,14,1..., dimensions={0} | all-to-all | bytes 458752 | tf_op jit(solution)/shard_map/all_to_all | solution.py:507
  83.0 0.8 finish.1
  (11 shorter events, 0.2 us)
Async XLA Ops:
  2.3 18.6 %collective-permute-start.2 = (bf16[384,256]{1,0:T(8,128)(2,1)S(1)}, bf16[384,256]{1,0:T(8,128)(2,1)S(1)}, u32[]{:S(2)}, u32[]{:S(2)}) collective-permute-start(bf16[384,256]{1,0:T(8,128)(2,1)S(1)} %get-tuple-element.26), channel_id=1, source_target_pairs={{8,16},{24,32},{40,48},{56,64},{72,80},{88,96},{104,112},{120,128}... | collective-permute-start | bytes 589832 | tf_op jit(solution)/shard_map/ppermute | solution.py:412
  7.6 8.0 %collective-permute-start = (bf16[384,384]{1,0:T(8,128)(2,1)S(1)}, bf16[384,384]{1,0:T(8,128)(2,1)S(1)}, u32[]{:S(2)}, u32[]{:S(2)}) collective-permute-start(bf16[384,384]{1,0:T(8,128)(2,1)S(1)} %get-tuple-element.22), channel_id=1, source_target_pairs={{8,16},{24,32},{40,48},{56,64},{72,80},{88,96},{104,112},{120,128}... | collective-permute-start | bytes 884744 | tf_op jit(solution)/shard_map/ppermute | solution.py:410
  9.6 6.1 %collective-permute-start.1 = (bf16[384,640]{1,0:T(8,128)(2,1)S(1)}, bf16[384,640]{1,0:T(8,128)(2,1)S(1)}, u32[]{:S(2)}, u32[]{:S(2)}) collective-permute-start(bf16[384,640]{1,0:T(8,128)(2,1)S(1)} %get-tuple-element.23), channel_id=1, source_target_pairs={{0,8},{16,24},{32,40},{48,56},{64,72},{80,88},{96,104},{112,120},{... | collective-permute-start | bytes 1474568 | tf_op jit(solution)/shard_map/ppermute | solution.py:411

commit v6 on v5

--- a/solution.py
+++ b/solution.py
@@ -31,13 +31,19 @@
 
 
 def pack_kernel(
-    x_hbm, g_hbm, nv_hbm, proj_hbm, own_ref, far_ref, far_g_ref, near_ref, m_ref, x_in, g_in, nv_in,
-    proj_in, flat_ref, sems,
+    x_hbm, g_hbm, nv_hbm, proj_hbm, mix_hbm, own_ref, far_ref, near_ref, m_ref, proj_ref, mix_ref,
+    x_in, g_in, nv_in, flat_ref, sems,
 ):
     copies = [
         pltpu.make_async_copy(source, target, sems.at[i])
         for i, (source, target) in enumerate(
-            ((x_hbm, x_in), (g_hbm, g_in), (nv_hbm, nv_in), (proj_hbm, proj_in))
+            (
+                (x_hbm, x_in),
+                (g_hbm, g_in),
+                (nv_hbm, nv_in),
+                (proj_hbm, proj_ref),
+                (mix_hbm, mix_ref),
+            )
         )
     ]
     for copy in copies:
@@ -57,7 +63,7 @@
         3.0
         * jnp.dot(
             nv_in[...],
-            block_diagonal(proj_in[...]),
+            block_diagonal(proj_ref[...]),
             precision=HIGHEST,
             preferred_element_type=F32,
         )
@@ -66,10 +72,9 @@
     own_ref[:, :width] = learned.astype(BF16)
     odd = lax.rem(lax.axis_index("node"), 2)
     gap = nodes - rim
-    far_rows = pl.ds(pl.multiple_of(odd * gap, BLOCK), rim)
-    far_ref[...] = own_ref[far_rows, : 3 * width]
-    far_g_ref[...] = own_ref[far_rows, 3 * width :]
+    far_ref[...] = own_ref[pl.ds(pl.multiple_of(odd * gap, BLOCK), rim), :]
     near_ref[...] = own_ref[pl.ds(pl.multiple_of((1 - odd) * gap, BLOCK), rim), :]
+    copies[4].wait()
 
 
 def unit_rows(first, count=1):
@@ -102,53 +107,63 @@
     return jnp.dot(learned, turn.astype(BF16), preferred_element_type=F32).astype(BF16)
 
 
-def forward_kernel(
+def layer_kernel(
     norm_scale,
     region_ref,
     first_ref,
     far_ref,
     near_ref,
     own_ref,
-    mix_hbm,
-    out_ref,
+    m_ref,
+    proj_ref,
+    mix_ref,
+    out_hbm,
     sums_ref,
+    x_ref,
+    g_ref,
+    learned_ref,
     swapped_ref,
-    x_ref,
-    one_ref,
-    prop_one_ref,
-    prop_two_ref,
+    adj_ref,
     adjt_ref,
     score_ref,
     rdeg_ref,
-    learned_ref,
-    adj_ref,
+    one_ref,
     two_ref,
+    q_one_ref,
+    q_two_ref,
+    back_ref,
+    off_ref,
+    offrow_ref,
+    dm_ref,
     flat_ref,
-    mix_ref,
+    out_ref,
     sem,
 ):
-    mix_copy = pltpu.make_async_copy(mix_hbm, mix_ref, sem)
-    mix_copy.start()
     b = BLOCK
     nodes = own_ref.shape[0]
-    rim, width = far_ref.shape[0], far_ref.shape[1] // 3
+    rim, width = far_ref.shape[0], m_ref.shape[1]
     own_units = nodes // b
     units = own_units + 2 * HALO
     reach = HALO + 1
+    row = 2 * width
+    keep = 1.0 - KEEP_INPUT
     far_place, near_place = rim_places(rim, nodes)
     own_place = pl.ds(rim, nodes)
     for place, source in ((far_place, far_ref), (own_place, own_ref), (near_place, near_ref)):
         learned = source[:, :width]
         learned_ref[place, :] = learned
         swapped_ref[place, :] = turned(learned)
-        x_ref[place, :] = source[:, width : 3 * width]
+        x_ref[place, :] = source[:, width : width + row]
+        g_ref[place, :] = source[:, width + row :]
 
     firsts = [first_ref[u] for u in range(units)]
+    windows = [pl.ds(pl.multiple_of(firsts[u] * b, b), reach * b) for u in range(units)]
     eye = (
         lax.broadcasted_iota(jnp.int32, (b, b), 0) == lax.broadcasted_iota(jnp.int32, (b, b), 1)
     ).astype(F32)
     own_first = HALO
     own_last = own_first + own_units
+    mixed = jnp.concatenate([mix_ref[2], mix_ref[1]], axis=0)
     for u in range(units):
         rows = unit_rows(u)
         mine = region_ref[u]
@@ -173,34 +188,51 @@
             adjt_ref[rows, columns] = (negative * negative).astype(BF16)
             total = total + forward
         degree = 1.0 + jnp.sum(total, axis=1, keepdims=True)
-        rdeg_ref[rows, :] = jnp.broadcast_to(1.0 / degree, (b, width))
+        rdeg = jnp.broadcast_to(1.0 / degree, (b, width))
+        rdeg_ref[rows, :] = rdeg
+        for s in range(2):
+            cut = slice(s * width, (s + 1) * width)
+            back = lax.dot_general(g_ref[rows, cut], mixed, NT, preferred_element_type=F32)
+            q_two_ref[rows, cut] = (keep * back[:, :width] * rdeg).astype(BF16)
+            back_ref[rows, cut] = back[:, width:]
     for u in range(units):
         rows = unit_rows(u)
         diagonal = pl.ds(pl.multiple_of((u - firsts[u]) * b, b), b)
         adj_ref[rows, diagonal] = (adj_ref[rows, diagonal].astype(F32) + eye).astype(BF16)
         adjt_ref[rows, diagonal] = (adjt_ref[rows, diagonal].astype(F32) + eye).astype(BF16)
 
-    keep = 1.0 - KEEP_INPUT
-    windows = [pl.ds(pl.multiple_of(firsts[u] * b, b), reach * b) for u in range(units)]
-    for u in range(units):
+    order = list(range(own_first, own_last))
+    order += [u for u in range(units) if u not in order]
+    for u in order:
         rows = unit_rows(u)
-        prop = jnp.dot(
-            adj_ref[rows, :], x_ref[windows[u], :], preferred_element_type=F32
-        ) * twice(rdeg_ref[rows, :])
-        prop_one_ref[rows, :] = prop.astype(BF16)
+        rdeg = twice(rdeg_ref[rows, :])
+        carried = jnp.dot(
+            adjt_ref[rows, :], q_two_ref[windows[u], :], preferred_element_type=F32
+        )
+        prop = jnp.dot(adj_ref[rows, :], x_ref[windows[u], :], preferred_element_type=F32) * rdeg
         one_ref[rows, :] = (KEEP_INPUT * x_ref[rows, :].astype(F32) + keep * prop).astype(BF16)
-    for u in range(units):
+        grad_one = (keep * (back_ref[rows, :] + carried) * rdeg).astype(BF16)
+        q_one_ref[rows, :] = grad_one
+        inner = grad_one.astype(F32) * prop
+        off_ref[rows, :] = inner[:, :width] + inner[:, width:]
+
+    def second_hop(u):
         rows = unit_rows(u)
         prop = jnp.dot(
             adj_ref[rows, :], one_ref[windows[u], :], preferred_element_type=F32
         ) * twice(rdeg_ref[rows, :])
-        prop_two_ref[rows, :] = prop.astype(BF16)
+        inner = q_two_ref[rows, :].astype(F32) * prop
+        inner = off_ref[rows, :] + inner[:, :width] + inner[:, width:]
+        offset = jnp.broadcast_to(jnp.sum(inner, axis=1, keepdims=True), (b, width))
+        off_ref[rows, :] = offset
+        offrow_ref[u] = jnp.transpose(offset)[:8]
         if own_first <= u < own_last:
             two_ref[unit_rows(u - own_first), :] = (
                 KEEP_INPUT * x_ref[rows, :].astype(F32) + keep * prop
             ).astype(BF16)
 
-    mix_copy.wait()
+    for u in range(own_first, own_last):
+        second_hop(u)
     weights = jnp.concatenate([mix_ref[0], mix_ref[1], mix_ref[2]], axis=0)
     all_hops, all_up = [], []
     for s in range(2):
@@ -210,95 +242,29 @@
                 [x_ref[own_place, cut], one_ref[own_place, cut], two_ref[:, cut]], axis=1
             )
         )
-        all_up.append(own_ref[:, 3 * width + s * width : 3 * width + (s + 1) * width])
+        all_up.append(g_ref[own_place, cut])
         flat_ref[pl.ds(s, nodes, stride=2), :] = jnp.dot(
             all_hops[s], weights, preferred_element_type=F32
         )
     out_ref[...] = flat_ref[...].astype(BF16)
-    sums_ref[...] = norm_scale * lax.dot_general(
+    out_copy = pltpu.make_async_copy(out_ref, out_hbm, sem)
+    out_copy.start()
+    for u in range(units):
+        if not own_first <= u < own_last:
+            second_hop(u)
+    groups = sums_ref.shape[0]
+    rows_v = nodes // groups
+    rows_w = 3 * width // groups
+    weight = norm_scale * lax.dot_general(
         jnp.concatenate(all_hops, axis=0),
         jnp.concatenate(all_up, axis=0),
         TN,
         preferred_element_type=F32,
     )
-
-
-def backward_kernel(
-    first_ref,
-    far_g_ref,
-    near_ref,
-    own_ref,
-    m_ref,
-    proj_hbm,
-    mix_hbm,
-    weight_ref,
-    swapped_ref,
-    x_ref,
-    one_ref,
-    prop_one_ref,
-    prop_two_ref,
-    adjt_ref,
-    score_ref,
-    rdeg_ref,
-    sums_ref,
-    g_ref,
-    q_one_ref,
-    q_two_ref,
-    back_ref,
-    off_ref,
-    offrow_ref,
-    dm_ref,
-    mix_ref,
-    proj_ref,
-    sems,
-):
-    copies = (
-        pltpu.make_async_copy(mix_hbm, mix_ref, sems.at[0]),
-        pltpu.make_async_copy(proj_hbm, proj_ref, sems.at[1]),
-    )
-    for copy in copies:
-        copy.start()
-    b = BLOCK
-    nodes, width = m_ref.shape
-    rim = far_g_ref.shape[0]
-    own_units = nodes // b
-    units = own_units + 2 * HALO
-    reach = HALO + 1
-    keep = 1.0 - KEEP_INPUT
-    far_place, near_place = rim_places(rim, nodes)
-    g_ref[far_place, :] = far_g_ref[...]
-    g_ref[near_place, :] = near_ref[:, 3 * width :]
-    g_ref[rim : rim + nodes, :] = own_ref[:, 3 * width :]
-    firsts = [first_ref[u] for u in range(units)]
-    windows = [pl.ds(pl.multiple_of(firsts[u] * b, b), reach * b) for u in range(units)]
-    for copy in copies:
-        copy.wait()
-    mixed = jnp.concatenate([mix_ref[2], mix_ref[1]], axis=0)
-    for r in range(0, units, 2):
-        rows = unit_rows(r, 2)
-        for s in range(2):
-            cut = slice(s * width, (s + 1) * width)
-            back = lax.dot_general(g_ref[rows, cut], mixed, NT, preferred_element_type=F32)
-            q_two_ref[rows, cut] = (
-                keep * back[:, :width] * rdeg_ref[rows, :]
-            ).astype(BF16)
-            back_ref[rows, cut] = back[:, width:]
-    for u in range(units):
-        rows = unit_rows(u)
-        carried = jnp.dot(
-            adjt_ref[rows, :], q_two_ref[windows[u], :], preferred_element_type=F32
-        )
-        grad_one = (keep * (back_ref[rows, :] + carried) * twice(rdeg_ref[rows, :])).astype(BF16)
-        q_one_ref[rows, :] = grad_one
-        inner = grad_one.astype(F32) * prop_one_ref[rows, :].astype(F32) + q_two_ref[
-            rows, :
-        ].astype(F32) * prop_two_ref[rows, :].astype(F32)
-        offset = jnp.broadcast_to(jnp.sum(inner, axis=1, keepdims=True), (b, width))
-        off_ref[rows, :] = offset
-        offrow_ref[u] = jnp.transpose(offset)[:8]
-
-    own_first = HALO
-    for u in range(own_first, own_first + own_units):
+    for k in range(groups):
+        sums_ref[k, rows_v:, :] = weight[k * rows_w : (k + 1) * rows_w].astype(BF16)
+
+    for u in range(own_first, own_last):
         rows = unit_rows(u)
         local = unit_rows(u - own_first)
         grad_m = jnp.zeros((b, width), F32)
@@ -336,12 +302,9 @@
         precision=HIGHEST,
         preferred_element_type=F32,
     ).astype(BF16)
-    groups = sums_ref.shape[0]
-    rows_v = nodes // groups
-    rows_w = weight_ref.shape[0] // groups
     for k in range(groups):
         sums_ref[k, :rows_v, :] = grad[k * rows_v : (k + 1) * rows_v]
-        sums_ref[k, rows_v:, :] = weight_ref[k * rows_w : (k + 1) * rows_w].astype(BF16)
+    out_copy.wait()
 
 
 def finish_kernel(got_ref, vector_ref, weight_ref):
@@ -383,33 +346,31 @@
         pltpu.with_memory_space_constraint(array, pltpu.HBM)
         for array in (features, cotangent, node_vectors, projections, mix_weight)
     )
-    own, far, far_g, near, learned = pl.pallas_call(
+    own, far, near, learned, projections, mix_weight = pl.pallas_call(
         pack_kernel,
         name="pack",
-        in_specs=[in_hbm] * 4,
+        in_specs=[in_hbm] * 5,
         out_shape=(
             jax.ShapeDtypeStruct((nodes, 5 * width), BF16),
-            jax.ShapeDtypeStruct((rim, 3 * width), BF16),
-            jax.ShapeDtypeStruct((rim, 2 * width), BF16),
+            jax.ShapeDtypeStruct((rim, 5 * width), BF16),
             jax.ShapeDtypeStruct((rim, 5 * width), BF16),
             jax.ShapeDtypeStruct((nodes, width), F32),
+            jax.ShapeDtypeStruct(projections.shape, F32),
+            jax.ShapeDtypeStruct(mix_weight.shape, BF16),
         ),
         scratch_shapes=[
             pltpu.VMEM((flat, width), BF16),
             pltpu.VMEM((flat, width), BF16),
             pltpu.VMEM((nodes, width), F32),
-            pltpu.VMEM(projections.shape, F32),
             pltpu.VMEM((flat, width), F32),
-            pltpu.SemaphoreType.DMA((4,)),
+            pltpu.SemaphoreType.DMA((5,)),
         ],
         compiler_params=pltpu.CompilerParams(vmem_limit_bytes=16 << 20),
-    )(features, cotangent, node_vectors, projections)
+    )(features, cotangent, node_vectors, projections, mix_weight)
     border = [(i, i + 1) for i in range(1, node_count - 1, 2)]
     inside = [(i, i + 1) for i in range(0, node_count, 2)]
-    across = border + [(j, i) for i, j in border]
-    far = lax.ppermute(far, "node", across)
     near = lax.ppermute(near, "node", inside + [(j, i) for i, j in inside])
-    far_g = lax.ppermute(far_g, "node", across)
+    far = lax.ppermute(far, "node", border + [(j, i) for i, j in border])
     lead = lax.axis_index("node") * own_units - HALO
     place = jnp.arange(units, dtype=jnp.int32)
     unit = lead + place
@@ -428,57 +389,41 @@
     rows_w = 3 * width // groups
     reach = (HALO + 1) * BLOCK
     in_smem = pl.BlockSpec(memory_space=pltpu.SMEM)
-    out, weights, *kept = pl.pallas_call(
-        partial(forward_kernel, 1.0 / math.sqrt(flat * node_count * win_count)),
-        name="forward",
-        in_specs=[in_smem] * 2 + [in_vmem] * 3 + [in_hbm],
+    out, sums = pl.pallas_call(
+        partial(layer_kernel, 1.0 / math.sqrt(flat * node_count * win_count)),
+        name="layer",
+        in_specs=[in_smem] * 2 + [in_vmem] * 6,
+        out_specs=(in_hbm, in_vmem),
         out_shape=(
             jax.ShapeDtypeStruct((flat, width), BF16),
-            jax.ShapeDtypeStruct((3 * width, width), F32),
-            jax.ShapeDtypeStruct((span, width), BF16),
-            jax.ShapeDtypeStruct((span, row), BF16),
-            jax.ShapeDtypeStruct((span, row), BF16),
-            jax.ShapeDtypeStruct((span, row), BF16),
-            jax.ShapeDtypeStruct((span, row), BF16),
-            jax.ShapeDtypeStruct((span, reach), BF16),
-            jax.ShapeDtypeStruct((nodes, reach), F32),
-            jax.ShapeDtypeStruct((span, width), F32),
+            jax.ShapeDtypeStruct((groups, rows_v + rows_w, width), BF16),
         ),
         scratch_shapes=[
+            pltpu.VMEM((span, row), BF16),
+            pltpu.VMEM((span, row), BF16),
+            pltpu.VMEM((span, width), BF16),
             pltpu.VMEM((span, width), BF16),
             pltpu.VMEM((span, reach), BF16),
+            pltpu.VMEM((span, reach), BF16),
+            pltpu.VMEM((nodes, reach), F32),
+            pltpu.VMEM((span, width), F32),
+            pltpu.VMEM((span, row), BF16),
             pltpu.VMEM((nodes, row), BF16),
-            pltpu.VMEM((flat, width), F32),
-            pltpu.VMEM(mix_weight.shape, BF16),
-            pltpu.SemaphoreType.DMA,
-        ],
-        compiler_params=pltpu.CompilerParams(vmem_limit_bytes=24 << 20),
-        cost_estimate=pl.CostEstimate(
-            flops=6 * span * reach * row, bytes_accessed=8 << 20, transcendentals=span * reach
-        ),
-    )(region, first, far, near, own, mix_weight)
-    sums = pl.pallas_call(
-        backward_kernel,
-        name="backward",
-        in_specs=[in_smem] + [in_vmem] * 4 + [in_hbm] * 2 + [in_vmem] * 9,
-        out_shape=jax.ShapeDtypeStruct((groups, rows_v + rows_w, width), BF16),
-        scratch_shapes=[
-            pltpu.VMEM((span, row), BF16),
             pltpu.VMEM((span, row), BF16),
             pltpu.VMEM((span, row), BF16),
             pltpu.VMEM((span, row), F32),
             pltpu.VMEM((span, width), F32),
             pltpu.VMEM((units, 8, width), F32),
             pltpu.VMEM((nodes, width), F32),
-            pltpu.VMEM(mix_weight.shape, BF16),
-            pltpu.VMEM(projections.shape, F32),
-            pltpu.SemaphoreType.DMA((2,)),
+            pltpu.VMEM((flat, width), F32),
+            pltpu.VMEM((flat, width), BF16),
+            pltpu.SemaphoreType.DMA,
         ],
-        compiler_params=pltpu.CompilerParams(vmem_limit_bytes=24 << 20),
+        compiler_params=pltpu.CompilerParams(vmem_limit_bytes=32 << 20),
         cost_estimate=pl.CostEstimate(
-            flops=6 * span * reach * row, bytes_accessed=8 << 20, transcendentals=0
+            flops=12 * span * reach * row, bytes_accessed=8 << 20, transcendentals=span * reach
         ),
-    )(first, far_g, near, own, learned, projections, mix_weight, weights, *kept)
+    )(region, first, far, near, own, learned, projections, mix_weight)
 
     counts = (y_far, y_near, inner_count, win_count)
     outer_groups = device_groups(counts, (0, 3))

time: 84.2 us -> 80.1 us (0.951)
  Pallas kernels: 12.9 us -> 9.79 us
    pallas_call x3 -> x2, Pallas kernels: 12.1 us -> 9 us  [the longest x1 7.36 us: body(): pl.pallas_call(partial(layer_kernel, 1.0 / math.sqrt(flat * node_count *...]
    ppermute x2 -> x1, starting transfers between devices: 7.29 us -> 5.37 us  [body(): far = lax.ppermute(far, 'node', border + [(j, i) for i, j in border])]
    ppermute x1, starting transfers between devices: 2.8 us -> 4.06 us  [body(): near = lax.ppermute(near, 'node', inside + [(j, i) for i, j in inside])]
    all_to_all x1, blocking collectives: 18.8 us -> 20 us  [body(): got = exchange(shares, axis_index_groups=inner_groups).astype(F32)]
    all_to_all x1, blocking collectives: 23.4 us -> 22.5 us  [body(): got = exchange(sums, axis_index_groups=outer_groups).astype(F32)]
  transfers between devices with their start and end apart: 3 -> 2, of which waited for: 1 -> 1; matrix products, arithmetic and copies ran while one was open for 2% -> 1% of each run, Pallas kernels for 6% -> 0%
where the time goes in v6:
time: 80.1 us; the launch traced here: 79.8 us
  blocking collectives  57.2 us (71%)
  Pallas kernels  9.79 us (12%)
  starting transfers between devices  9.43 us (12%)
  waiting for transfers between devices  1.17 us (1%)
  local copies, waits for them, and re-layouts  0.82 us (1%)
    all_to_all x1, blocking collectives, body(): got = exchange(sums, axis_index_groups=outer_groups).astype(F32)  22.5 us
    all_to_all x1, blocking collectives, body(): got = exchange(shares, axis_index_groups=inner_groups).astype(F32)  20 us
    all_to_all x1, blocking collectives, body(): got = exchange(back, axis_index_groups=outer_groups)  14.7 us
    pallas_call x1, Pallas kernels, body(): pl.pallas_call(partial(layer_kernel, 1.0 / math.sqrt(flat * node_count *...  7.36 us
    ppermute x1, starting transfers between devices, body(): far = lax.ppermute(far, 'node', border + [(j, i) for i, j in border])  5.37 us
    ppermute x1, starting transfers between devices, body(): near = lax.ppermute(near, 'node', inside + [(j, i) for i, j in inside])  4.06 us
    pallas_call x1, Pallas kernels, body(): pl.pallas_call(pack_kernel, name='pack', in_specs=[in_hbm] * 5, out_shape...  1.64 us
  transfers between devices with their start and end apart: 2, of which 1 were waited for; matrix products, arithmetic and copies ran while one was open for 1% of the time, Pallas kernels for 0%

profile of v6, /device:TPU:1, one launch (start us, length us, event | category | flops | bytes accessed | tf_op | source)
XLA Modules:
  0.0 79.8 jit_solution(12053653191887066061)
XLA Ops:
  0.6 1.6 %pack.1 = (bf16[512,640]{1,0:T(8,128)(2,1)S(1)}, bf16[384,640]{1,0:T(8,128)(2,1)S(1)}, bf16[384,640]{1,0:T(8,128)(2,1)S(1)}, f32[512,128]{1,0:T(8,128)S(1)}, f32...) custom-call(bf16[1024,128]{1,0:T(8,128)(2,1)} %bitcast.11, bf16[1024,128]{1,0:T(8,128)(2,1)} %bitcast.12, ...), custom_call_target="tpu_custom_call" | custom-call | tf_op jit(solution)/shard_map/pack/pallas_call | solution.py:349
  2.3 5.4 %collective-permute-start = (bf16[384,640]{1,0:T(8,128)(2,1)S(1)}, bf16[384,640]{1,0:T(8,128)(2,1)S(1)}, u32[]{:S(2)}, u32[]{:S(2)}) collective-permute-start(bf16[384,640]{1,0:T(8,128)(2,1)S(1)} %get-tuple-element.15), channel_id=1, source_target_pairs={{8,16},{24,32},{40,48},{56,64},{72,80},{88,96},{104,112},{120,128}... | collective-permute-start | bytes 1474568 | tf_op jit(solution)/shard_map/ppermute | solution.py:373
  7.7 4.1 %collective-permute-start.1 = (bf16[384,640]{1,0:T(8,128)(2,1)S(1)}, bf16[384,640]{1,0:T(8,128)(2,1)S(1)}, u32[]{:S(2)}, u32[]{:S(2)}) collective-permute-start(bf16[384,640]{1,0:T(8,128)(2,1)S(1)} %get-tuple-element.16), channel_id=1, source_target_pairs={{0,8},{16,24},{32,40},{48,56},{64,72},{80,88},{96,104},{112,120},{... | collective-permute-start | bytes 1474568 | tf_op jit(solution)/shard_map/ppermute | solution.py:372
  11.7 0.0 copy-start
  11.7 0.6 copy-done
  12.4 0.1 copy.13
  12.5 0.2 reduce-window.8
  12.7 0.1 reduce.1
  12.8 0.2 fusion.1
  13.0 1.2 %collective-permute-done.far_ref = bf16[384,640]{1,0:T(8,128)(2,1)S(1)} collective-permute-done((bf16[384,640]{1,0:T(8,128)(2,1)S(1)}, bf16[384,640]{1,0:T(8,128)(2,1)S(1)}, u32[]{:S(2)}, u32[]{:S(2)}) %collective-permute-start) | collective-permute-done | bytes 491552 | tf_op jit(solution)/shard_map/ppermute | solution.py:373
  14.2 0.0 collective-permute-done.1.near_ref
  14.2 7.4 %layer.1 = (bf16[1024,128]{1,0:T(8,128)(2,1)}, bf16[16,56,128]{2,1,0:T(8,128)(2,1)S(1)}) custom-call(s32[10]{0:T(128)S(1)} %get-tuple-element.38.region_ref, s32[10]{0:T(128)S(1)} %get-tuple-element.39.first_ref, bf16[384,640]{1,0:T(8,128)(2,1)S(1)} %collective-permute-done.far_ref, bf16[384,640]{1,0:T(8,128)(2,1)S(1)} %collective-permute-done.1.near_ref, ...), custom_call_target="tpu_custom_call" | custom-call | flops 2013265920 | bytes 8388608 | tf_op jit(solution)/shard_map/layer/pallas_call | solution.py:392
  21.5 22.5 %all_to_all.15 = bf16[16,56,128]{2,1,0:T(8,128)(2,1)S(1)} all-to-all(bf16[16,56,128]{2,1,0:T(8,128)(2,1)S(1)} %get-tuple-element.22), channel_id=1, replica_groups={{0,1,2,3,4,5,6,7,256,257,258,259,260,261,262,263},{8,9,10,11,12,13,14,1..., dimensions={0} | all-to-all | bytes 458752 | tf_op jit(solution)/shard_map/all_to_all | solution.py:434
  44.1 20.0 %all_to_all.16 = bf16[32,24,128]{2,1,0:T(8,128)(2,1)S(1)} all-to-all(bf16[32,24,128]{2,1,0:T(8,128)(2,1)S(1)} %broadcast_in_dim.11), channel_id=1, replica_groups={{0,8,16,24,32,40,48,56,64,72,80,88,96,104,112,120,128,136,144,152,160,1..., dimensions={0} | all-to-all | bytes 393216 | tf_op jit(solution)/shard_map/all_to_all | solution.py:441
  64.3 14.7 %all_to_all.17.got_ref = bf16[16,56,128]{2,1,0:T(8,128)(2,1)S(1)} all-to-all(bf16[16,56,128]{2,1,0:T(8,128)(2,1)S(1)} %pad_maximum_fusion), channel_id=1, replica_groups={{0,1,2,3,4,5,6,7,256,257,258,259,260,261,262,263},{8,9,10,11,12,13,14,1..., dimensions={0} | all-to-all | bytes 458752 | tf_op jit(solution)/shard_map/all_to_all | solution.py:452
  79.0 0.8 finish.1
  (10 shorter events, 0.2 us)
Async XLA Ops:
  2.3 11.9 %collective-permute-start = (bf16[384,640]{1,0:T(8,128)(2,1)S(1)}, bf16[384,640]{1,0:T(8,128)(2,1)S(1)}, u32[]{:S(2)}, u32[]{:S(2)}) collective-permute-start(bf16[384,640]{1,0:T(8,128)(2,1)S(1)} %get-tuple-element.15), channel_id=1, source_target_pairs={{8,16},{24,32},{40,48},{56,64},{72,80},{88,96},{104,112},{120,128}... | collective-permute-start | bytes 1474568 | tf_op jit(solution)/shard_map/ppermute | solution.py:373
  7.7 6.5 %collective-permute-start.1 = (bf16[384,640]{1,0:T(8,128)(2,1)S(1)}, bf16[384,640]{1,0:T(8,128)(2,1)S(1)}, u32[]{:S(2)}, u32[]{:S(2)}) collective-permute-start(bf16[384,640]{1,0:T(8,128)(2,1)S(1)} %get-tuple-element.16), channel_id=1, source_target_pairs={{0,8},{16,24},{32,40},{48,56},{64,72},{80,88},{96,104},{112,120},{... | collective-permute-start | bytes 1474568 | tf_op jit(solution)/shard_map/ppermute | solution.py:372
  11.7 0.7 copy-start

commit v7 on v6

--- a/solution.py
+++ b/solution.py
@@ -158,9 +158,6 @@
 
     firsts = [first_ref[u] for u in range(units)]
     windows = [pl.ds(pl.multiple_of(firsts[u] * b, b), reach * b) for u in range(units)]
-    eye = (
-        lax.broadcasted_iota(jnp.int32, (b, b), 0) == lax.broadcasted_iota(jnp.int32, (b, b), 1)
-    ).astype(F32)
     own_first = HALO
     own_last = own_first + own_units
     mixed = jnp.concatenate([mix_ref[2], mix_ref[1]], axis=0)
@@ -195,12 +192,6 @@
             back = lax.dot_general(g_ref[rows, cut], mixed, NT, preferred_element_type=F32)
             q_two_ref[rows, cut] = (keep * back[:, :width] * rdeg).astype(BF16)
             back_ref[rows, cut] = back[:, width:]
-    for u in range(units):
-        rows = unit_rows(u)
-        diagonal = pl.ds(pl.multiple_of((u - firsts[u]) * b, b), b)
-        adj_ref[rows, diagonal] = (adj_ref[rows, diagonal].astype(F32) + eye).astype(BF16)
-        adjt_ref[rows, diagonal] = (adjt_ref[rows, diagonal].astype(F32) + eye).astype(BF16)
-
     order = list(range(own_first, own_last))
     order += [u for u in range(units) if u not in order]
     for u in order:
@@ -209,8 +200,11 @@
         carried = jnp.dot(
             adjt_ref[rows, :], q_two_ref[windows[u], :], preferred_element_type=F32
         )
-        prop = jnp.dot(adj_ref[rows, :], x_ref[windows[u], :], preferred_element_type=F32) * rdeg
-        one_ref[rows, :] = (KEEP_INPUT * x_ref[rows, :].astype(F32) + keep * prop).astype(BF16)
+        mine = x_ref[rows, :].astype(F32)
+        prop = jnp.dot(adj_ref[rows, :], x_ref[windows[u], :], preferred_element_type=F32)
+        prop = (prop + mine) * rdeg
+        one_ref[rows, :] = (KEEP_INPUT * mine + keep * prop).astype(BF16)
+        carried = carried + q_two_ref[rows, :].astype(F32)
         grad_one = (keep * (back_ref[rows, :] + carried) * rdeg).astype(BF16)
         q_one_ref[rows, :] = grad_one
         inner = grad_one.astype(F32) * prop
@@ -218,9 +212,8 @@
 
     def second_hop(u):
         rows = unit_rows(u)
-        prop = jnp.dot(
-            adj_ref[rows, :], one_ref[windows[u], :], preferred_element_type=F32
-        ) * twice(rdeg_ref[rows, :])
+        prop = jnp.dot(adj_ref[rows, :], one_ref[windows[u], :], preferred_element_type=F32)
+        prop = (prop + one_ref[rows, :].astype(F32)) * twice(rdeg_ref[rows, :])
         inner = q_two_ref[rows, :].astype(F32) * prop
         inner = off_ref[rows, :] + inner[:, :width] + inner[:, width:]
         offset = jnp.broadcast_to(jnp.sum(inner, axis=1, keepdims=True), (b, width))
@@ -369,8 +362,8 @@
     )(features, cotangent, node_vectors, projections, mix_weight)
     border = [(i, i + 1) for i in range(1, node_count - 1, 2)]
     inside = [(i, i + 1) for i in range(0, node_count, 2)]
+    far = lax.ppermute(far, "node", border + [(j, i) for i, j in border])
     near = lax.ppermute(near, "node", inside + [(j, i) for i, j in inside])
-    far = lax.ppermute(far, "node", border + [(j, i) for i, j in border])
     lead = lax.axis_index("node") * own_units - HALO
     place = jnp.arange(units, dtype=jnp.int32)
     unit = lead + place
@@ -379,7 +372,9 @@
     in_range = (unit >= 0) & (unit < node_count * own_units)
     region = jnp.where(in_range, jnp.sum(passed, axis=1), -1)
     first = jnp.sum(passed * region_sizes[None, :], axis=1) - lead
-    first = jnp.clip(first, jnp.maximum(place - HALO, 0), jnp.minimum(place, units - HALO - 1))
+    first = jnp.clip(
+        first, jnp.maximum(place - HALO, 0), jnp.minimum(place, units - HALO - 1)
+    )
 
     span = units * BLOCK
     y_far, y_near = 2, 2

time: 80.1 us -> 79.7 us (level)
  no operation moved by 1% of the time
where the time goes in v7:
time: 79.7 us; the launch traced here: 79.4 us
  blocking collectives  57.2 us (72%)
  starting transfers between devices  9.43 us (12%)
  Pallas kernels  9.41 us (12%)
  waiting for transfers between devices  1.17 us (1%)
  local copies, waits for them, and re-layouts  0.82 us (1%)
    all_to_all x1, blocking collectives, body(): got = exchange(sums, axis_index_groups=outer_groups).astype(F32)  22.5 us
    all_to_all x1, blocking collectives, body(): got = exchange(shares, axis_index_groups=inner_groups).astype(F32)  20 us
    all_to_all x1, blocking collectives, body(): got = exchange(back, axis_index_groups=outer_groups)  14.7 us
    pallas_call x1, Pallas kernels, body(): pl.pallas_call(partial(layer_kernel, 1.0 / math.sqrt(flat * node_count *...  6.98 us
    ppermute x1, starting transfers between devices, body(): far = lax.ppermute(far, 'node', border + [(j, i) for i, j in border])  5.37 us
    ppermute x1, starting transfers between devices, body(): near = lax.ppermute(near, 'node', inside + [(j, i) for i, j in inside])  4.06 us
    pallas_call x1, Pallas kernels, body(): pl.pallas_call(pack_kernel, name='pack', in_specs=[in_hbm] * 5, out_shape...  1.64 us
  transfers between devices with their start and end apart: 2, of which 1 were waited for; matrix products, arithmetic and copies ran while one was open for 1% of the time, Pallas kernels for 0%

profile of v7, /device:TPU:1, one launch (start us, length us, event | category | flops | bytes accessed | tf_op | source)
XLA Modules:
  0.0 79.4 jit_solution(12358101558358420308)
XLA Ops:
  0.6 1.6 %pack.1 = (bf16[512,640]{1,0:T(8,128)(2,1)S(1)}, bf16[384,640]{1,0:T(8,128)(2,1)S(1)}, bf16[384,640]{1,0:T(8,128)(2,1)S(1)}, f32[512,128]{1,0:T(8,128)S(1)}, f32...) custom-call(bf16[1024,128]{1,0:T(8,128)(2,1)} %bitcast.11, bf16[1024,128]{1,0:T(8,128)(2,1)} %bitcast.12, ...), custom_call_target="tpu_custom_call" | custom-call | tf_op jit(solution)/shard_map/pack/pallas_call | solution.py:342
  2.3 5.4 %collective-permute-start = (bf16[384,640]{1,0:T(8,128)(2,1)S(1)}, bf16[384,640]{1,0:T(8,128)(2,1)S(1)}, u32[]{:S(2)}, u32[]{:S(2)}) collective-permute-start(bf16[384,640]{1,0:T(8,128)(2,1)S(1)} %get-tuple-element.15), channel_id=1, source_target_pairs={{8,16},{24,32},{40,48},{56,64},{72,80},{88,96},{104,112},{120,128}... | collective-permute-start | bytes 1474568 | tf_op jit(solution)/shard_map/ppermute | solution.py:365
  7.7 4.1 %collective-permute-start.1 = (bf16[384,640]{1,0:T(8,128)(2,1)S(1)}, bf16[384,640]{1,0:T(8,128)(2,1)S(1)}, u32[]{:S(2)}, u32[]{:S(2)}) collective-permute-start(bf16[384,640]{1,0:T(8,128)(2,1)S(1)} %get-tuple-element.16), channel_id=1, source_target_pairs={{0,8},{16,24},{32,40},{48,56},{64,72},{80,88},{96,104},{112,120},{... | collective-permute-start | bytes 1474568 | tf_op jit(solution)/shard_map/ppermute | solution.py:366
  11.7 0.0 copy-start
  11.7 0.6 copy-done
  12.4 0.1 copy.13
  12.5 0.2 reduce-window.8
  12.7 0.1 reduce.1
  12.8 0.2 fusion.1
  13.0 1.2 %collective-permute-done.far_ref = bf16[384,640]{1,0:T(8,128)(2,1)S(1)} collective-permute-done((bf16[384,640]{1,0:T(8,128)(2,1)S(1)}, bf16[384,640]{1,0:T(8,128)(2,1)S(1)}, u32[]{:S(2)}, u32[]{:S(2)}) %collective-permute-start) | collective-permute-done | bytes 491552 | tf_op jit(solution)/shard_map/ppermute | solution.py:365
  14.2 0.0 collective-permute-done.1.near_ref
  14.2 7.0 %layer.1 = (bf16[1024,128]{1,0:T(8,128)(2,1)}, bf16[16,56,128]{2,1,0:T(8,128)(2,1)S(1)}) custom-call(s32[10]{0:T(128)S(1)} %get-tuple-element.38.region_ref, s32[10]{0:T(128)S(1)} %get-tuple-element.39.first_ref, bf16[384,640]{1,0:T(8,128)(2,1)S(1)} %collective-permute-done.far_ref, bf16[384,640]{1,0:T(8,128)(2,1)S(1)} %collective-permute-done.1.near_ref, ...), custom_call_target="tpu_custom_call" | custom-call | flops 2013265920 | bytes 8388608 | tf_op jit(solution)/shard_map/layer/pallas_call | solution.py:387
  21.1 22.5 %all_to_all.15 = bf16[16,56,128]{2,1,0:T(8,128)(2,1)S(1)} all-to-all(bf16[16,56,128]{2,1,0:T(8,128)(2,1)S(1)} %get-tuple-element.22), channel_id=1, replica_groups={{0,1,2,3,4,5,6,7,256,257,258,259,260,261,262,263},{8,9,10,11,12,13,14,1..., dimensions={0} | all-to-all | bytes 458752 | tf_op jit(solution)/shard_map/all_to_all | solution.py:429
  43.8 20.0 %all_to_all.16 = bf16[32,24,128]{2,1,0:T(8,128)(2,1)S(1)} all-to-all(bf16[32,24,128]{2,1,0:T(8,128)(2,1)S(1)} %broadcast_in_dim.11), channel_id=1, replica_groups={{0,8,16,24,32,40,48,56,64,72,80,88,96,104,112,120,128,136,144,152,160,1..., dimensions={0} | all-to-all | bytes 393216 | tf_op jit(solution)/shard_map/all_to_all | solution.py:436
  63.9 14.7 %all_to_all.17.got_ref = bf16[16,56,128]{2,1,0:T(8,128)(2,1)S(1)} all-to-all(bf16[16,56,128]{2,1,0:T(8,128)(2,1)S(1)} %pad_maximum_fusion), channel_id=1, replica_groups={{0,1,2,3,4,5,6,7,256,257,258,259,260,261,262,263},{8,9,10,11,12,13,14,1..., dimensions={0} | all-to-all | bytes 458752 | tf_op jit(solution)/shard_map/all_to_all | solution.py:447
  78.6 0.8 finish.1
  (10 shorter events, 0.2 us)
Async XLA Ops:
  2.3 11.9 %collective-permute-start = (bf16[384,640]{1,0:T(8,128)(2,1)S(1)}, bf16[384,640]{1,0:T(8,128)(2,1)S(1)}, u32[]{:S(2)}, u32[]{:S(2)}) collective-permute-start(bf16[384,640]{1,0:T(8,128)(2,1)S(1)} %get-tuple-element.15), channel_id=1, source_target_pairs={{8,16},{24,32},{40,48},{56,64},{72,80},{88,96},{104,112},{120,128}... | collective-permute-start | bytes 1474568 | tf_op jit(solution)/shard_map/ppermute | solution.py:365
  7.7 6.5 %collective-permute-start.1 = (bf16[384,640]{1,0:T(8,128)(2,1)S(1)}, bf16[384,640]{1,0:T(8,128)(2,1)S(1)}, u32[]{:S(2)}, u32[]{:S(2)}) collective-permute-start(bf16[384,640]{1,0:T(8,128)(2,1)S(1)} %get-tuple-element.16), channel_id=1, source_target_pairs={{0,8},{16,24},{32,40},{48,56},{64,72},{80,88},{96,104},{112,120},{... | collective-permute-start | bytes 1474568 | tf_op jit(solution)/shard_map/ppermute | solution.py:366
  11.7 0.7 copy-start
